TPU v7x, 32 devices: a whole 2x2x4 slice. The times are simulated.
32 devices in a mesh: row: 2 (over y), col: 16 (over z, x, core).
Axes of the slice: x: 2, y: 2, z: 4, core: 2. Of those that a mesh axis runs over, the one named last changes fastest.
Arguments:
- side_a: float32 [16, 8192], P('row', 'col'), may hold values from -6 to 6
- side_b: float32 [512, 8192], P('col', 'row'), may hold values from -6 to 6
- pair_grad: float32 [16, 512, 128], P('row', 'col'), may hold values from -6 to 6
- out_weight: float32 [1024, 128], replicated, may hold values from -0.1875 to 0.1875
Outputs:
- grad_a: float32 [16, 8192], P('row', 'col')
- grad_b: float32 [512, 8192], P('col', 'row')
- grad_weight: float32 [1024, 128], replicated
- grad_bias: float32 [128], replicated
All inputs are finite; a program needn't handle non-finite values.
Results may differ from a plain program's by a relative error of at most 0.00013.
Values sent between devices are 32-bit elements; how exact they have to be, the bound alone decides.
No kernel may reach another device: no remote copies, remote signals or barrier semaphores. Data moves between devices by JAX's collectives and lax.ppermute only.
A program may use at most 64 MiB of HBM per device.

v0:
```python
import jax
import jax.numpy as jnp
from jax import lax
from jax.sharding import PartitionSpec as P

S = 256
C = 32
P_SIZE = 128


def local(side_a, side_b, pair_grad, out_weight):
    high = lax.Precision.HIGHEST
    rows = pair_grad.shape[0]
    cols = pair_grad.shape[1]
    left = lax.all_gather(side_a, "col", axis=1, tiled=True).reshape(rows, S, C)
    right = lax.all_gather(side_b, "row", axis=1, tiled=True).reshape(cols, S, C)
    left_flat = jnp.transpose(left, (0, 2, 1)).reshape(rows * C, S)
    right_flat = jnp.transpose(right, (1, 0, 2)).reshape(S, cols * C)
    flat_pair = pair_grad.reshape(rows * cols, P_SIZE)
    grad_outer = jnp.dot(flat_pair, out_weight.T, precision=high)
    grad_tile = jnp.transpose(grad_outer.reshape(rows, cols, C, C), (0, 2, 1, 3)).reshape(
        rows * C, cols * C
    )
    left_grad = jnp.dot(grad_tile, right_flat.T, precision=high) / S
    left_part = jnp.transpose(left_grad.reshape(rows, C, S), (0, 2, 1)).reshape(rows, S * C)
    right_grad = jnp.dot(left_flat.T, grad_tile, precision=high) / S
    right_part = jnp.transpose(right_grad.reshape(S, cols, C), (1, 0, 2)).reshape(cols, S * C)
    grad_a = lax.psum_scatter(left_part, "col", scatter_dimension=1, tiled=True)
    grad_b = lax.psum_scatter(right_part, "row", scatter_dimension=1, tiled=True)
    outer = jnp.dot(left_flat, right_flat, precision=high) / S
    outer = jnp.transpose(outer.reshape(rows, C, cols, C), (0, 2, 1, 3)).reshape(rows * cols, C * C)
    weight_part = jnp.dot(outer.T, flat_pair, precision=high)
    bias_part = jnp.sum(flat_pair, axis=0)
    weight_sums = lax.psum((weight_part, bias_part), ("row", "col"))
    return (grad_a, grad_b, weight_sums[0], weight_sums[1])


def solution(mesh):
    in_specs = (P("row", "col"), P("col", "row"), P("row", "col", None), P())
    out_specs = (P("row", "col"), P("col", "row"), P(), P())
    return jax.shard_map(local, mesh=mesh, in_specs=in_specs, out_specs=out_specs, check_vma=False)
```

profile of v0, /device:TPU:0, one launch (start us, length us, event | category | flops | bytes accessed | tf_op | source)
XLA Modules:
  0.0 286.0 jit_solution(1570294501840764260)
XLA Ops:
  7.2 0.7 all-gather.2.cloned.1.call-update
  8.2 5.9 %convolution_bitcast_fusion = f32[8,32,32,32]{3,2,1,0:T(8,128)} fusion(f32[32,32,128,1]{2,1,0,3:T(8,128)S(1)} %bitcast.37, f32[8,32,128]{2,1,0:T(8,128)} %param.6), kind=kOutput, calls=%fused_computation.1 | convolution fusion | flops 402653184 | bytes 1703936 | tf_op jit(solution)/shard_map/dot_general | solution.py:20
  14.1 3.7 %reshape.48 = f32[256,1024]{1,0:T(8,128)S(1)} reshape(f32[8,32,32,32]{3,2,1,0:T(8,128)} %convolution_bitcast_fusion) | data formatting | bytes 2097152 | tf_op jit(solution)/shard_map/reshape | solution.py:21
  17.9 24.0 %all_gather.7 = f32[8,8192]{1,0:T(8,128)S(1)} all-gather(f32[8,512]{1,0:T(8,128)S(1)} %copy-done.2), channel_id=1, replica_groups=mesh['row'=2,'col'=16] {'col'}, dimensions={1}, use_global_device_ids=true | all-gather | bytes 278528 | tf_op jit(solution)/shard_map/all_gather | solution.py:15
  41.9 0.3 reshape.53
  42.3 0.3 copy.12
  42.6 3.7 %reshape.49 = f32[32,256,32]{2,1,0:T(8,128)} reshape(f32[32,8192]{1,0:T(8,128)} %all-gather.2.cloned.1.call-done) | data formatting | bytes 2097152 | tf_op jit(solution)/shard_map/reshape | solution.py:16
  46.3 2.8 copy.10
  49.1 2.0 convolution_multiply_fusion
  51.1 3.9 %reshape.57 = f32[8,32,32,32]{3,2,1,0:T(8,128)} reshape(f32[256,1024]{1,0:T(8,128)} %convolution_multiply_fusion) | data formatting | bytes 2097152 | tf_op jit(solution)/shard_map/reshape | solution.py:31
  55.1 6.5 %copy.17 = f32[8,32,32,32]{3,1,2,0:T(8,128)} copy(f32[8,32,32,32]{3,2,1,0:T(8,128)} %reshape.57) | data formatting | bytes 2097152 | tf_op jit(solution)/shard_map/reshape | solution.py:31
  61.6 4.6 %reshape.58 = f32[256,1024]{1,0:T(8,128)} reshape(f32[8,32,32,32]{3,2,1,0:T(8,128)} %bitcast.40) | data formatting | bytes 2097152 | tf_op jit(solution)/shard_map/reshape | solution.py:31
  66.2 3.8 %fusion.1 = f32[1024,128]{1,0:T(8,128)} fusion(f32[256,1024]{1,0:T(8,128)} %reshape.58, f32[256,128]{1,0:T(8,128)S(1)} %bitcast.48), kind=kOutput, calls=%fused_computation.6 | convolution fusion | flops 402653184 | bytes 1703936 | tf_op jit(solution)/shard_map/dot_general | solution.py:32
  70.1 1.0 convolution_multiply_fusion.2
  71.1 0.3 copy.11
  71.5 1.2 reshape.52
  73.0 1.8 convolution_multiply_fusion.1
  74.8 2.7 copy.13
  77.5 4.3 %reshape.56 = f32[32,8192]{1,0:T(8,128)} reshape(f32[32,256,32]{2,1,0:T(8,128)} %bitcast.39) | data formatting | bytes 2097152 | tf_op jit(solution)/shard_map/reshape | solution.py:27
  81.9 37.0 %psum.15 = f32[128]{0:T(128)} all-reduce(f32[128]{0:T(128)S(1)} %reduce_sum.9), channel_id=1, replica_groups=mesh['row'=2,'col'=16] {'row','col'}, use_global_device_ids=true, to_apply=%region_4.0 | all-reduce | flops 128 | bytes 1024 | tf_op jit(solution)/shard_map/psum | solution.py:34
  118.9 77.7 %all-reduce.2.cloned.1.call-done = f32[1024,128]{1,0:T(8,128)} async-done(((f32[1024,128]{1,0:T(8,128)}), f32[1024,128]{1,0:T(8,128)}) %all-reduce.2.cloned.1.call-update) | async-done | bytes 524304 | tf_op jit(solution)/shard_map/psum | solution.py:34
  196.6 58.9 %reduce-scatter.3.cloned.1.call-done = f32[8,512]{1,0:T(8,128)} async-done(((f32[8,8192]{1,0:T(8,128)}), f32[8,512]{1,0:T(8,128)}) %reduce-scatter.3.cloned.1.call-update) | async-done | bytes 16400 | tf_op jit(solution)/shard_map/reduce_scatter | solution.py:28
  255.5 22.1 %reduce-scatter.5.cloned.1.call-done = f32[32,4096]{1,0:T(8,128)} async-done(((f32[32,8192]{1,0:T(8,128)}), f32[32,4096]{1,0:T(8,128)}) %reduce-scatter.5.cloned.1.call-update) | async-done | bytes 524304 | tf_op jit(solution)/shard_map/reduce_scatter | solution.py:29
  277.6 1.9 copy.19
  (15 shorter events, 0.8 us)
Async XLA Ops:
  7.2 1.0 copy-start
  7.2 35.4 %all-gather.2.cloned.1.call-start = ((), (), s32[]{:S(2)}) async-start(), calls=%async_computation.2 | async-start | bytes 1572864 | tf_op jit(solution)/shard_map/all_gather | solution.py:16
  7.9 188.7 %all-reduce.2.cloned.1.call-start = ((), (), s32[]{:S(2)}) async-start(), calls=%async_computation.5 | async-start | bytes 1048576 | tf_op jit(solution)/shard_map/psum | solution.py:34
  8.2 9.7 %copy-start.2 = (f32[8,512]{1,0:T(8,128)S(1)}, f32[8,512]{1,0:T(8,128)}, u32[]{:S(2)}) copy-start(f32[8,512]{1,0:T(8,128)} %param.4) | copy-start | bytes 49156
  61.6 4.6 %copy-start.1 = (f32[8,32,128]{2,1,0:T(8,128)S(1)}, f32[8,32,128]{2,1,0:T(8,128)}, u32[]{:S(2)}) copy-start(f32[8,32,128]{2,1,0:T(8,128)} %param.6) | copy-start | bytes 393220
  70.1 185.4 %reduce-scatter.3.cloned.1.call-start = ((), (), s32[]{:S(2)}) async-start(), calls=%async_computation.3 | async-start | bytes 278528 | tf_op jit(solution)/shard_map/reduce_scatter | solution.py:28
  72.7 204.9 %reduce-scatter.5.cloned.1.call-start = ((), (), s32[]{:S(2)}) async-start(), calls=%async_computation.4 | async-start | bytes 1572864 | tf_op jit(solution)/shard_map/reduce_scatter | solution.py:29
Sparse Core Ops, SparseCore 0:
  9.5 23.9 all-gather.1
  70.2 126.3 all-reduce.1
  200.7 54.7 reduce-scatter.2
  258.2 19.4 reduce-scatter.4
where the time goes:
time: 287 us; the launch traced here: 286 us
  waiting for transfers between devices  160 us (56%)
  blocking collectives  61 us (21%)
  local copies, waits for them, and re-layouts  36.7 us (13%)
  matrix products  14.6 us (5%)
  between operations  13.8 us (5%)
    psum x1, waiting for transfers between devices, local(): weight_sums = lax.psum((weight_part, bias_part), ('row', 'col'))  77.7 us
    reduce_scatter x1, waiting for transfers between devices, local(): grad_a = lax.psum_scatter(left_part, 'col', scatter_dimension=1, tiled=True)  58.9 us
    psum x1, blocking collectives, local(): weight_sums = lax.psum((weight_part, bias_part), ('row', 'col'))  37 us
    all_gather x1, blocking collectives, local(): left = lax.all_gather(side_a, 'col', axis=1, tiled=True).reshape(rows, S, C)  24 us
    reduce_scatter x1, waiting for transfers between devices, local(): lax.psum_scatter(right_part, 'row', scatter_dimension=1, tiled=True)  22.1 us
    reshape x2, local copies, waits for them, and re-layouts, local(): outer.reshape(rows, C, cols, C)  10.4 us
    dot_general x1, matrix products, local(): grad_outer = jnp.dot(flat_pair, out_weight.T, precision=high)  5.9 us
  transfers between devices with their start and end apart: 4, of which 3 were waited for; matrix products, arithmetic and copies ran while one was open for 8% of the time, Pallas kernels for 0%

commit v1 on v0

v1 whole, which is shorter than its diff:
```python
import math

import jax
import jax.numpy as jnp
from jax import lax
from jax.experimental import pallas as pl
from jax.experimental.pallas import tpu as pltpu
from jax.sharding import PartitionSpec as P

LANES = 128
NT = (((1,), (1,)), ((), ()))
NN = (((1,), (0,)), ((), ()))


def split(x):
    hi = x.astype(jnp.bfloat16)
    lo = (x - hi.astype(jnp.float32)).astype(jnp.bfloat16)
    return hi, lo


def dot3(a, b, dims):
    def one(u, v):
        return lax.dot_general(u, v, dims, preferred_element_type=jnp.float32)

    return one(a[0], b[0]) + (one(a[0], b[1]) + one(a[1], b[0]))


def swap_blocks(parts):
    n = len(parts)
    width = LANES // n
    block = lax.broadcasted_iota(jnp.int32, parts[0].shape, 1) // width
    step = 1
    while step < n:
        low = (block & step) == 0
        done = list(parts)
        for t in range(n):
            if t & step == 0:
                p, r = parts[t], parts[t + step]
                done[t] = jnp.where(low, p, pltpu.roll(r, step * width, 1))
                done[t + step] = jnp.where(low, pltpu.roll(p, LANES - step * width, 1), r)
        parts = done
        step *= 2
    return parts


def place(m, order):
    p = 0
    for k, bit in enumerate(order):
        p = p | (((m >> bit) & 1) << k)
    return p


class Dims:
    def __init__(self, mesh, side_a, side_b, pair_grad, out_weight):
        self.R, self.Q = mesh.shape["row"], mesh.shape["col"]
        self.rows, self.cols, self.K = pair_grad.shape
        self.CE = out_weight.shape[0]
        self.C = math.isqrt(self.CE)
        self.S = side_a.shape[1] * self.Q // self.C
        self.n = LANES // self.C
        self.G = self.C // self.n
        self.slab = self.S // self.R
        self.g = self.slab // self.n
        self.blk = side_a.shape[1]
        self.gb = self.blk // LANES
        self.per = self.Q // self.R
        self.IC = self.rows * self.C
        self.JE = self.cols * self.C


def first_kernel(d, pg_ref, w_ref, b_ref, gh_ref, gl_ref, bh_ref, bl_ref, t_ref, tb_ref):
    pg = split(pg_ref[...].reshape(d.rows * d.cols, d.K))
    pairs = d.rows * d.cols
    two = 2 if d.G % 2 == 0 else 1
    for u in range(0, d.G, two):
        w = jnp.concatenate(
            [w_ref[pl.ds((p4 * d.G + v) * d.C, d.C), :] for v in range(u, u + two) for p4 in range(d.n)], axis=0
        )
        out = dot3(pg, split(w), NT)
        for v in range(two):
            t_ref[pl.ds((u + v) * pairs, pairs), :] = out[:, v * LANES:(v + 1) * LANES]

    def body(i, carry):
        for quad in range(d.cols // d.n):
            parts = [t_ref[pl.ds(i * d.cols + quad * d.n + t, d.G, stride=pairs), :] for t in range(d.n)]
            hi, lo = split(jnp.concatenate(swap_blocks(parts), axis=0))
            at = pl.multiple_of(i * d.C, d.C)
            gh_ref[pl.ds(at, d.C), quad * LANES:(quad + 1) * LANES] = hi
            gl_ref[pl.ds(at, d.C), quad * LANES:(quad + 1) * LANES] = lo
        return carry

    lax.fori_loop(0, d.rows, body, 0)
    to_seq(d, b_ref, bh_ref, bl_ref, 0, tb_ref)


def to_seq(d, b_ref, bh_ref, bl_ref, at, tb_ref):
    for v in range(d.g):
        tb_ref[pl.ds(v * d.cols, d.cols), :] = b_ref[:, v * LANES:(v + 1) * LANES]
    for quad in range(d.cols // d.n):
        parts = [tb_ref[pl.ds(quad * d.n + t, d.g, stride=d.cols), :] for t in range(d.n)]
        hi, lo = split(jnp.concatenate(swap_blocks(parts), axis=0))
        bh_ref[at:at + d.slab, quad * LANES:(quad + 1) * LANES] = hi
        bl_ref[at:at + d.slab, quad * LANES:(quad + 1) * LANES] = lo


def second_kernel(d, order, blocks, pg_ref, a_ref, bx_ref, bh_ref, bl_ref, w_ref, ah_ref, al_ref, xh_ref, xl_ref,
                  t_ref, tb_ref, ta_ref, o_ref):
    r, q = lax.axis_index("row"), lax.axis_index("col")
    pairs = d.rows * d.cols
    xh_ref[0:d.slab, :] = bh_ref[...]
    xl_ref[0:d.slab, :] = bl_ref[...]
    for m in range(1, d.R):
        to_seq(d, bx_ref.at[m - 1], xh_ref, xl_ref, m * d.slab, tb_ref)
    for m in range(d.R):
        for k in range(d.per):
            src = place(((r ^ m) * d.per + k) ^ q, order)
            for v in range(d.gb):
                ta_ref[pl.ds((k * d.gb + v) * d.rows, d.rows), :] = a_ref[src, :, v * LANES:(v + 1) * LANES]
        for quad in range(d.rows // d.n):
            parts = [ta_ref[pl.ds(quad * d.n + t, d.g, stride=d.rows), :] for t in range(d.n)]
            o_ref[m * d.slab:(m + 1) * d.slab, quad * LANES:(quad + 1) * LANES] = jnp.concatenate(
                swap_blocks(parts), axis=0) * (1.0 / d.S)
    a = o_ref[0:d.S, 0:d.IC]
    hi, lo = split(a)
    ah_ref[...] = hi
    al_ref[...] = lo
    o_ref[0:d.IC, :] = dot3(split(a.T), (xh_ref[...], xl_ref[...]), NN)

    def body(i, carry):
        for quad in range(d.cols // d.n):
            parts = [o_ref[pl.ds(pl.multiple_of(i * d.C + p4 * d.G, d.G), d.G), quad * LANES:(quad + 1) * LANES]
                     for p4 in range(d.n)]
            for t, x in enumerate(swap_blocks(parts)):
                t_ref[pl.ds(i * d.cols + quad * d.n + t, d.G, stride=pairs), :] = x
        return carry

    lax.fori_loop(0, d.rows, body, 0)
    flat = pg_ref[...].reshape(pairs, d.K)
    turned = split(flat.T)
    beta = blocks.mine()
    per = d.CE // blocks.count
    for u in range(d.G):
        part = dot3(turned, split(t_ref[pl.ds(u * pairs, pairs), :]), NN).T
        for p4 in range(d.n):
            row = (p4 * d.G + u) * d.C
            w_ref[(row // per) ^ beta, pl.ds(row % per, d.C), :] = part[p4 * d.C:(p4 + 1) * d.C]
    bias = jnp.broadcast_to(jnp.sum(flat, axis=0, keepdims=True), (8, d.K))
    for t in range(blocks.count):
        w_ref[t, pl.ds(per, 8), :] = bias


def third_kernel(d, order, gh_ref, gl_ref, ah_ref, al_ref, xh_ref, xl_ref, gb_ref, ga_ref, tb_ref, ta_ref, o_ref):
    r, q = lax.axis_index("row"), lax.axis_index("col")
    gt = gh_ref[...], gl_ref[...]
    for m in range(d.R):
        at = slice(m * d.slab, (m + 1) * d.slab)
        o_ref[0:d.slab, :] = dot3((ah_ref[at, :], al_ref[at, :]), gt, NN)
        for quad in range(d.cols // d.n):
            parts = [o_ref[p * d.g:(p + 1) * d.g, quad * LANES:(quad + 1) * LANES] for p in range(d.n)]
            for t, x in enumerate(swap_blocks(parts)):
                tb_ref[pl.ds(quad * d.n + t, d.g, stride=d.cols), :] = x
        for v in range(d.g):
            gb_ref[m, :, v * LANES:(v + 1) * LANES] = tb_ref[pl.ds(v * d.cols, d.cols), :]
    for m in range(d.R):
        at = slice(m * d.slab, (m + 1) * d.slab)
        out = dot3((xh_ref[at, :], xl_ref[at, :]), gt, NT) * (1.0 / d.S)
        for quad in range(d.rows // d.n):
            parts = [out[p * d.g:(p + 1) * d.g, quad * LANES:(quad + 1) * LANES] for p in range(d.n)]
            for t, x in enumerate(swap_blocks(parts)):
                ta_ref[pl.ds(quad * d.n + t, d.g, stride=d.rows), :] = x
        for k in range(d.per):
            dst = place(((r ^ m) * d.per + k) ^ q, order)
            for v in range(d.gb):
                ga_ref[dst, :, v * LANES:(v + 1) * LANES] = ta_ref[pl.ds((k * d.gb + v) * d.rows, d.rows), :]


def last_kernel(blocks, per, mine_ref, other_ref, w_ref, bias_ref):
    beta = blocks.mine()
    half = blocks.count // 2
    for t in range(half):
        at = pl.multiple_of((t ^ beta) * per, per)
        w_ref[pl.ds(at, per), :] = mine_ref[t, 0:per, :]
        at = pl.multiple_of(((t + half) ^ beta) * per, per)
        w_ref[pl.ds(at, per), :] = other_ref[t, 0:per, :]
    bias_ref[...] = mine_ref[0, per:per + 8, :]


def swap_with(x, axis, bit, size):
    return lax.ppermute(x, axis, [(i, i ^ (1 << bit)) for i in range(size)])


class Blocks:
    def __init__(self, bits):
        self.bits = bits
        self.count = 1 << len(bits)

    def mine(self):
        p = 0
        for axis, bit in self.bits:
            p = (p << 1) | ((lax.axis_index(axis) >> bit) & 1)
        return p


def call(kernel, outs, scratch, *args):
    return pl.pallas_call(
        kernel,
        out_shape=outs,
        scratch_shapes=[pltpu.VMEM(s, jnp.float32) for s in scratch],
        compiler_params=pltpu.CompilerParams(vmem_limit_bytes=48 << 20),
    )(*args)


def shape(*dims, dtype=jnp.float32):
    return jax.ShapeDtypeStruct(dims, dtype)


def build(mesh):
    size = {"row": mesh.shape["row"], "col": mesh.shape["col"]}
    count = {axis: n.bit_length() - 1 for axis, n in size.items()}
    order = list(range(2, count["col"])) + [b for b in (1, 0) if b < count["col"]]

    def local(side_a, side_b, pair_grad, out_weight):
        d = Dims(mesh, side_a, side_b, pair_grad, out_weight)
        half = jnp.bfloat16
        taken = [("col", 0), ("col", 1), ("row", 0)]
        rest = [(x, b) for x in ("col", "row") for b in range(count[x]) if (x, b) not in taken]
        blocks = Blocks(taken)
        pairs = d.rows * d.cols
        t_s, tb_s, ta_s = (d.G * pairs, LANES), (d.g * d.cols, LANES), (d.g * d.rows, LANES)
        o_s = (max(d.S, d.IC), d.JE)

        right = side_b[None]
        for bit in range(count["row"]):
            right = jnp.concatenate([right, swap_with(right, "row", bit, d.R)])
        left = side_a[None]
        for bit in order:
            left = jnp.concatenate([left, swap_with(left, "col", bit, d.Q)])

        big, small = shape(d.IC, d.JE, dtype=half), shape(d.slab, d.JE, dtype=half)
        gh, gl, bh, bl = call(
            lambda *refs: first_kernel(d, *refs), [big, big, small, small], [t_s, tb_s], pair_grad, out_weight, side_b
        )
        amat, bmat = shape(d.S, d.IC, dtype=half), shape(d.S, d.JE, dtype=half)
        per = d.CE // blocks.count
        part, ah, al, xh, xl = call(
            lambda *refs: second_kernel(d, order, blocks, *refs),
            [shape(blocks.count, per + 8, d.K), amat, amat, bmat, bmat],
            [t_s, tb_s, ta_s, o_s],
            pair_grad, left, right[1:], bh, bl,
        )
        gb, ga = call(
            lambda *refs: third_kernel(d, order, *refs),
            [shape(d.R, d.cols, d.slab * d.C), shape(d.Q, d.rows, d.blk)],
            [tb_s, ta_s, (d.slab, d.JE)],
            gh, gl, ah, al, xh, xl,
        )
        for axis, bit in taken:
            n = part.shape[0] // 2
            part = part[:n] + swap_with(part[n:], axis, bit, size[axis])
        for axis, bit in rest:
            part = part + swap_with(part, axis, bit, size[axis])
        for axis, bit in taken[:0:-1]:
            part = jnp.concatenate([part, swap_with(part, axis, bit, size[axis])])
        other = swap_with(part, *taken[0], size[taken[0][0]])
        weight, bias = call(
            lambda *refs: last_kernel(blocks, per, *refs), [shape(d.CE, d.K), shape(8, d.K)], [], part, other
        )
        for bit in range(count["row"] - 1, -1, -1):
            n = gb.shape[0] // 2
            gb = gb[:n] + swap_with(gb[n:], "row", bit, d.R)
        for bit in order[::-1]:
            n = ga.shape[0] // 2
            ga = ga[:n] + swap_with(ga[n:], "col", bit, d.Q)
        return ga[0], gb[0], weight, bias[0]

    return local


def solution(mesh):
    in_specs = (P("row", "col"), P("col", "row"), P("row", "col", None), P())
    out_specs = (P("row", "col"), P("col", "row"), P(), P())
    return jax.shard_map(build(mesh), mesh=mesh, in_specs=in_specs, out_specs=out_specs, check_vma=False)
```

time: 287 us -> 67.2 us (0.23)
  waiting for transfers between devices: 160 us -> 27.7 us
  blocking collectives: 61 us -> 0 us
  local copies, waits for them, and re-layouts: 36.7 us -> 3.63 us
  starting transfers between devices: 0.38 us -> 22.4 us
  matrix products: 14.6 us -> 0 us
  between operations: 13.8 us -> 0.83 us
  Pallas kernels: 0 us -> 10 us
    reduce_scatter x2 -> x0, waiting for transfers between devices: 81 us -> none  [the longest x1 58.9 us: local(): grad_a = lax.psum_scatter(left_part, 'col', scatter_dimension=1, tiled=True)]
    psum x1 -> x0, waiting for transfers between devices: 77.7 us -> none  [local(): weight_sums = lax.psum((weight_part, bias_part), ('row', 'col'))]
    psum x1 -> x0, blocking collectives: 37 us -> none  [local(): weight_sums = lax.psum((weight_part, bias_part), ('row', 'col'))]
    reshape x10 -> x0, local copies, waits for them, and re-layouts: 31.4 us -> none  [the longest x2 10.4 us: local(): outer.reshape(rows, C, cols, C)]
    ppermute x0 -> x18, waiting for transfers between devices: none -> 27.7 us  [swap_with(): return lax.ppermute(x, axis, [(i, i ^ 1 << bit) for i in range(size)])]
    all_gather x1 -> x0, blocking collectives: 24 us -> none  [local(): left = lax.all_gather(side_a, 'col', axis=1, tiled=True).reshape(rows, S, C)]
    ppermute x0 -> x18, starting transfers between devices: none -> 22.4 us  [swap_with(): return lax.ppermute(x, axis, [(i, i ^ 1 << bit) for i in range(size)])]
    dot_general x5 -> x0, matrix products: 14.6 us -> none  [the longest x1 5.9 us: local(): grad_outer = jnp.dot(flat_pair, out_weight.T, precision=high)]
  transfers between devices with their start and end apart: 4 -> 18, of which waited for: 3 -> 13; matrix products, arithmetic and copies ran while one was open for 8% -> 4% of each run, Pallas kernels for 0% -> 8%
where the time goes in v1:
time: 67.2 us; the launch traced here: 66.9 us
  waiting for transfers between devices  27.7 us (41%)
  starting transfers between devices  22.4 us (33%)
  Pallas kernels  10 us (15%)
  local copies, waits for them, and re-layouts  3.63 us (5%)
  other arithmetic  2.37 us (4%)
  between operations  0.83 us (1%)
    ppermute x18, waiting for transfers between devices, swap_with(): return lax.ppermute(x, axis, [(i, i ^ 1 << bit) for i in range(size)])  27.7 us
    ppermute x18, starting transfers between devices, swap_with(): return lax.ppermute(x, axis, [(i, i ^ 1 << bit) for i in range(size)])  22.4 us
    pallas_call x4, Pallas kernels, call(): pl.pallas_call(kernel, out_shape=outs, scratch_shapes=[pltpu.VMEM(s, jnp....  10 us
    unnamed x12, local copies, waits for them, and re-layouts  3.01 us
    squeeze x2, other arithmetic, local(): return (ga[0], gb[0], weight, bias[0])  1.48 us
  transfers between devices with their start and end apart: 18, of which 13 were waited for; matrix products, arithmetic and copies ran while one was open for 4% of the time, Pallas kernels for 8%

profile of v1, /device:TPU:0, one launch (start us, length us, event | category | flops | bytes accessed | tf_op | source)
XLA Modules:
  0.0 66.9 jit_solution(6175884765003664224)
XLA Ops:
  0.6 3.1 %collective-permute-start = (f32[1,8,512]{2,1,0:T(8,128)}, f32[1,8,512]{2,1,0:T(8,128)S(1)}, u32[]{:S(2)}, u32[]{:S(2)}) collective-permute-start(f32[1,8,512]{2,1,0:T(8,128)} %bitcast.10), channel_id=1, source_target_pairs={{0,4},{1,5},{2,6},{3,7},{4,0},{5,1},{6,2},{7,3},{8,12},{9,13},{10,... | collective-permute-start | bytes 49160 | tf_op jit(solution)/shard_map/ppermute | solution.py:189
  3.8 1.5 %collective-permute-start.4 = (f32[1,32,4096]{2,1,0:T(8,128)}, f32[1,32,4096]{2,1,0:T(8,128)S(1)}, u32[]{:S(2)}, u32[]{:S(2)}) collective-permute-start(f32[1,32,4096]{2,1,0:T(8,128)} %bitcast.9), channel_id=1, source_target_pairs={{0,16},{16,0},{1,17},{17,1},{2,18},{18,2},{3,19},{19,3},{4,20},{20... | collective-permute-start | bytes 1572872 | tf_op jit(solution)/shard_map/ppermute | solution.py:189
  6.4 3.0 %collective-permute-start.1 = (f32[2,8,512]{2,1,0:T(8,128)S(1)}, f32[2,8,512]{2,1,0:T(8,128)S(1)}, u32[]{:S(2)}, u32[]{:S(2)}) collective-permute-start(f32[2,8,512]{2,1,0:T(8,128)S(1)} %pad_maximum_fusion.4), channel_id=1, source_target_pairs={{0,8},{1,9},{2,10},{3,11},{4,12},{5,13},{6,14},{7,15},{8,0},{9,1},... | collective-permute-start | bytes 98312 | tf_op jit(solution)/shard_map/ppermute | solution.py:189
  12.4 3.0 %shard_map.75 = (bf16[256,1024]{1,0:T(8,128)(2,1)S(1)}, bf16[256,1024]{1,0:T(8,128)(2,1)S(1)}, bf16[128,1024]{1,0:T(8,128)(2,1)S(1)}, bf16[128,1024]{1,0:T(8,128)(2,1)S(1)}) custom-call(f32[8,32,128]{2,1,0:T(8,128)S(1)} %copy-done.2, f32[1024,128]{1,0:T(8,128)S(1)} %copy-done, f32[32,4096]{1,0:T(8,128)S(1)} %copy-done.1), custom_call_target="tpu_custom_call" | custom-call | tf_op jit(solution)/shard_map/pallas_call | solution.py:205
  15.5 1.6 %collective-permute-start.2 = (f32[4,8,512]{2,1,0:T(8,128)S(1)}, f32[4,8,512]{2,1,0:T(8,128)S(1)}, u32[]{:S(2)}, u32[]{:S(2)}) collective-permute-start(f32[4,8,512]{2,1,0:T(8,128)S(1)} %pad_maximum_fusion.3), channel_id=1, source_target_pairs={{0,2},{1,3},{2,0},{3,1},{4,6},{5,7},{6,4},{7,5},{8,10},{9,11},{10,... | collective-permute-start | bytes 196616 | tf_op jit(solution)/shard_map/ppermute | solution.py:189
  17.0 2.8 %collective-permute-done.2 = f32[4,8,512]{2,1,0:T(8,128)S(1)} collective-permute-done((f32[4,8,512]{2,1,0:T(8,128)S(1)}, f32[4,8,512]{2,1,0:T(8,128)S(1)}, u32[]{:S(2)}, u32[]{:S(2)}) %collective-permute-start.2) | collective-permute-done | bytes 65568 | tf_op jit(solution)/shard_map/ppermute | solution.py:189
  19.9 1.3 %collective-permute-done.3 = f32[8,8,512]{2,1,0:T(8,128)S(1)} collective-permute-done((f32[8,8,512]{2,1,0:T(8,128)S(1)}, f32[8,8,512]{2,1,0:T(8,128)S(1)}, u32[]{:S(2)}, u32[]{:S(2)}) %collective-permute-start.3) | collective-permute-done | bytes 131104 | tf_op jit(solution)/shard_map/ppermute | solution.py:189
  21.2 3.7 %shard_map.76 = (f32[8,136,128]{2,1,0:T(8,128)S(1)}, bf16[256,256]{1,0:T(8,128)(2,1)S(1)}, bf16[256,256]{1,0:T(8,128)(2,1)S(1)}, bf16[256,1024]{1,0:T(8,128)(2,1)S(1)}, bf16[256,1024]{1,0:T(8,128)(2,1)S(1)}) custom-call(f32[8,32,128]{2,1,0:T(8,128)S(1)} %copy-done.2, f32[16,8,512]{2,1,0:T(8,128)S(1)} %constant_dynamic-update-slice_fusion.refs_1_, ...), custom_call_target="tpu_custom_call" | custom-call | tf_op jit(solution)/shard_map/pallas_call | solution.py:205
  25.2 1.4 %collective-permute-done.10 = f32[4,136,128]{2,1,0:T(8,128)S(1)} collective-permute-done((f32[4,136,128]{2,1,0:T(8,128)S(1)}, f32[4,136,128]{2,1,0:T(8,128)S(1)}, u32[]{:S(2)}, u32[]{:S(2)}) %collective-permute-start.10) | collective-permute-done | bytes 278560 | tf_op jit(solution)/shard_map/ppermute | solution.py:189
  26.6 1.6 %collective-permute-start.11 = (f32[2,136,128]{2,1,0:T(8,128)S(1)}, f32[2,136,128]{2,1,0:T(8,128)S(1)}, u32[]{:S(2)}, u32[]{:S(2)}) collective-permute-start(f32[2,136,128]{2,1,0:T(8,128)S(1)} %slice.75), channel_id=1, source_target_pairs={{0,2},{1,3},{2,0},{3,1},{4,6},{5,7},{6,4},{7,5},{8,10},{9,11},{10,... | collective-permute-start | bytes 417800 | tf_op jit(solution)/shard_map/ppermute | solution.py:189
  28.2 4.2 %collective-permute-done.11 = f32[2,136,128]{2,1,0:T(8,128)S(1)} collective-permute-done((f32[2,136,128]{2,1,0:T(8,128)S(1)}, f32[2,136,128]{2,1,0:T(8,128)S(1)}, u32[]{:S(2)}, u32[]{:S(2)}) %collective-permute-start.11) | collective-permute-done | bytes 139296 | tf_op jit(solution)/shard_map/ppermute | solution.py:189
  32.5 1.6 %collective-permute-start.12 = (f32[1,136,128]{2,1,0:T(8,128)S(1)}, f32[1,136,128]{2,1,0:T(8,128)S(1)}, u32[]{:S(2)}, u32[]{:S(2)}) collective-permute-start(f32[1,136,128]{2,1,0:T(8,128)S(1)} %slice.77), channel_id=1, source_target_pairs={{0,16},{16,0},{1,17},{17,1},{2,18},{18,2},{3,19},{19,3},{4,20},{20... | collective-permute-start | bytes 208904 | tf_op jit(solution)/shard_map/ppermute | solution.py:189
  34.0 2.5 %shard_map.77 = (f32[2,32,4096]{2,1,0:T(8,128)S(1)}, f32[16,8,512]{2,1,0:T(8,128)S(1)}) custom-call(bf16[256,1024]{1,0:T(8,128)(2,1)S(1)} %get-tuple-element.17.refs_0_, bf16[256,1024]{1,0:T(8,128)(2,1)S(1)} %get-tuple-element.18.refs_1_, bf16[256,256]{1,0:T(8,128)(2,1)S(1)} %get-tuple-element.21.refs_2_, bf16[256,256]{1,0:T(8,128)(2,1)S(1)} %get-tuple-element.22.refs_3_, ...), custom_call_target="tpu_custom_call" | custom-call | tf_op jit(solution)/shard_map/pallas_call | solution.py:205
  36.8 1.6 %collective-permute-start.13 = (f32[1,136,128]{2,1,0:T(8,128)S(1)}, f32[1,136,128]{2,1,0:T(8,128)S(1)}, u32[]{:S(2)}, u32[]{:S(2)}) collective-permute-start(f32[1,136,128]{2,1,0:T(8,128)S(1)} %slice_add_fusion.3), channel_id=1, source_target_pairs={{0,4},{1,5},{2,6},{3,7},{4,0},{5,1},{6,2},{7,3},{8,12},{9,13},{10,... | collective-permute-start | bytes 208904 | tf_op jit(solution)/shard_map/ppermute | solution.py:189
  38.5 1.6 %collective-permute-start.6 = (f32[4,8,512]{2,1,0:T(8,128)S(1)}, f32[4,8,512]{2,1,0:T(8,128)S(1)}, u32[]{:S(2)}, u32[]{:S(2)}) collective-permute-start(f32[4,8,512]{2,1,0:T(8,128)S(1)} %slice.69), channel_id=1, source_target_pairs={{0,2},{1,3},{2,0},{3,1},{4,6},{5,7},{6,4},{7,5},{8,10},{9,11},{10,... | collective-permute-start | bytes 196616 | tf_op jit(solution)/shard_map/ppermute | solution.py:189
  40.1 1.2 %collective-permute-done.13 = f32[1,136,128]{2,1,0:T(8,128)S(1)} collective-permute-done((f32[1,136,128]{2,1,0:T(8,128)S(1)}, f32[1,136,128]{2,1,0:T(8,128)S(1)}, u32[]{:S(2)}, u32[]{:S(2)}) %collective-permute-start.13) | collective-permute-done | bytes 69664 | tf_op jit(solution)/shard_map/ppermute | solution.py:189
  41.7 1.1 %collective-permute-done.6 = f32[4,8,512]{2,1,0:T(8,128)S(1)} collective-permute-done((f32[4,8,512]{2,1,0:T(8,128)S(1)}, f32[4,8,512]{2,1,0:T(8,128)S(1)}, u32[]{:S(2)}, u32[]{:S(2)}) %collective-permute-start.6) | collective-permute-done | bytes 65568 | tf_op jit(solution)/shard_map/ppermute | solution.py:189
  42.9 1.5 %collective-permute-start.7 = (f32[2,8,512]{2,1,0:T(8,128)S(1)}, f32[2,8,512]{2,1,0:T(8,128)S(1)}, u32[]{:S(2)}, u32[]{:S(2)}) collective-permute-start(f32[2,8,512]{2,1,0:T(8,128)S(1)} %slice.71), channel_id=1, source_target_pairs={{0,8},{1,9},{2,10},{3,11},{4,12},{5,13},{6,14},{7,15},{8,0},{9,1},... | collective-permute-start | bytes 98312 | tf_op jit(solution)/shard_map/ppermute | solution.py:189
  44.4 1.5 %collective-permute-start.9 = (f32[1,32,4096]{2,1,0:T(8,128)S(1)}, f32[1,32,4096]{2,1,0:T(8,128)S(1)}, u32[]{:S(2)}, u32[]{:S(2)}) collective-permute-start(f32[1,32,4096]{2,1,0:T(8,128)S(1)} %slice.60), channel_id=1, source_target_pairs={{0,16},{16,0},{1,17},{17,1},{2,18},{18,2},{3,19},{19,3},{4,20},{20... | collective-permute-start | bytes 1572872 | tf_op jit(solution)/shard_map/ppermute | solution.py:189
  45.9 2.7 %collective-permute-done.14 = f32[1,136,128]{2,1,0:T(8,128)S(1)} collective-permute-done((f32[1,136,128]{2,1,0:T(8,128)S(1)}, f32[1,136,128]{2,1,0:T(8,128)S(1)}, u32[]{:S(2)}, u32[]{:S(2)}) %collective-permute-start.14) | collective-permute-done | bytes 69664 | tf_op jit(solution)/shard_map/ppermute | solution.py:189
  49.0 1.3 %collective-permute-start.8 = (f32[1,8,512]{2,1,0:T(8,128)S(1)}, f32[1,8,512]{2,1,0:T(8,128)S(1)}, u32[]{:S(2)}, u32[]{:S(2)}) collective-permute-start(f32[1,8,512]{2,1,0:T(8,128)S(1)} %slice.73), channel_id=1, source_target_pairs={{0,4},{1,5},{2,6},{3,7},{4,0},{5,1},{6,2},{7,3},{8,12},{9,13},{10,... | collective-permute-start | bytes 49160 | tf_op jit(solution)/shard_map/ppermute | solution.py:189
  50.3 8.4 %collective-permute-done.15 = f32[1,136,128]{2,1,0:T(8,128)S(1)} collective-permute-done((f32[1,136,128]{2,1,0:T(8,128)S(1)}, f32[1,136,128]{2,1,0:T(8,128)S(1)}, u32[]{:S(2)}, u32[]{:S(2)}) %collective-permute-start.15) | collective-permute-done | bytes 69664 | tf_op jit(solution)/shard_map/ppermute | solution.py:189
  58.8 1.6 %collective-permute-start.16 = (f32[2,136,128]{2,1,0:T(8,128)S(1)}, f32[2,136,128]{2,1,0:T(8,128)S(1)}, u32[]{:S(2)}, u32[]{:S(2)}) collective-permute-start(f32[2,136,128]{2,1,0:T(8,128)S(1)} %pad_maximum_fusion.1), channel_id=1, source_target_pairs={{0,2},{1,3},{2,0},{3,1},{4,6},{5,7},{6,4},{7,5},{8,10},{9,11},{10,... | collective-permute-start | bytes 417800 | tf_op jit(solution)/shard_map/ppermute | solution.py:189
  60.9 2.9 %collective-permute-done.16 = f32[2,136,128]{2,1,0:T(8,128)S(1)} collective-permute-done((f32[2,136,128]{2,1,0:T(8,128)S(1)}, f32[2,136,128]{2,1,0:T(8,128)S(1)}, u32[]{:S(2)}, u32[]{:S(2)}) %collective-permute-start.16) | collective-permute-done | bytes 139296 | tf_op jit(solution)/shard_map/ppermute | solution.py:189
  (53 shorter events, 9.3 us)
Async XLA Ops:
  0.6 5.0 %collective-permute-start = (f32[1,8,512]{2,1,0:T(8,128)}, f32[1,8,512]{2,1,0:T(8,128)S(1)}, u32[]{:S(2)}, u32[]{:S(2)}) collective-permute-start(f32[1,8,512]{2,1,0:T(8,128)} %bitcast.10), channel_id=1, source_target_pairs={{0,4},{1,5},{2,6},{3,7},{4,0},{5,1},{6,2},{7,3},{8,12},{9,13},{10,... | collective-permute-start | bytes 49160 | tf_op jit(solution)/shard_map/ppermute | solution.py:189
  3.7 5.7 %copy-start.3 = (f32[8,512]{1,0:T(8,128)S(1)}, f32[8,512]{1,0:T(8,128)}, u32[]{:S(2)}) copy-start(f32[8,512]{1,0:T(8,128)} %param.4) | copy-start | bytes 49156
  3.8 17.5 %collective-permute-start.4 = (f32[1,32,4096]{2,1,0:T(8,128)}, f32[1,32,4096]{2,1,0:T(8,128)S(1)}, u32[]{:S(2)}, u32[]{:S(2)}) collective-permute-start(f32[1,32,4096]{2,1,0:T(8,128)} %bitcast.9), channel_id=1, source_target_pairs={{0,16},{16,0},{1,17},{17,1},{2,18},{18,2},{3,19},{19,3},{4,20},{20... | collective-permute-start | bytes 1572872 | tf_op jit(solution)/shard_map/ppermute | solution.py:189
  6.4 9.0 %collective-permute-start.1 = (f32[2,8,512]{2,1,0:T(8,128)S(1)}, f32[2,8,512]{2,1,0:T(8,128)S(1)}, u32[]{:S(2)}, u32[]{:S(2)}) collective-permute-start(f32[2,8,512]{2,1,0:T(8,128)S(1)} %pad_maximum_fusion.4), channel_id=1, source_target_pairs={{0,8},{1,9},{2,10},{3,11},{4,12},{5,13},{6,14},{7,15},{8,0},{9,1},... | collective-permute-start | bytes 98312 | tf_op jit(solution)/shard_map/ppermute | solution.py:189
  9.4 1.0 %copy-start = (f32[1024,128]{1,0:T(8,128)S(1)}, f32[1024,128]{1,0:T(8,128)}, u32[]{:S(2)}) copy-start(f32[1024,128]{1,0:T(8,128)} %refs_1_.1) | copy-start | bytes 1572868
  10.5 1.0 %copy-start.1 = (f32[32,4096]{1,0:T(8,128)S(1)}, f32[32,4096]{1,0:T(8,128)}, u32[]{:S(2)}) copy-start(f32[32,4096]{1,0:T(8,128)} %refs_2_.1) | copy-start | bytes 1572868
  11.5 0.9 %copy-start.2 = (f32[8,32,128]{2,1,0:T(8,128)S(1)}, f32[8,32,128]{2,1,0:T(8,128)}, u32[]{:S(2)}) copy-start(f32[8,32,128]{2,1,0:T(8,128)} %refs_0_.3) | copy-start | bytes 393220
  15.5 4.3 %collective-permute-start.2 = (f32[4,8,512]{2,1,0:T(8,128)S(1)}, f32[4,8,512]{2,1,0:T(8,128)S(1)}, u32[]{:S(2)}, u32[]{:S(2)}) collective-permute-start(f32[4,8,512]{2,1,0:T(8,128)S(1)} %pad_maximum_fusion.3), channel_id=1, source_target_pairs={{0,2},{1,3},{2,0},{3,1},{4,6},{5,7},{6,4},{7,5},{8,10},{9,11},{10,... | collective-permute-start | bytes 196616 | tf_op jit(solution)/shard_map/ppermute | solution.py:189
  19.8 1.4 %collective-permute-start.3 = (f32[8,8,512]{2,1,0:T(8,128)S(1)}, f32[8,8,512]{2,1,0:T(8,128)S(1)}, u32[]{:S(2)}, u32[]{:S(2)}) collective-permute-start(f32[8,8,512]{2,1,0:T(8,128)S(1)} %pad_maximum_fusion.2), channel_id=1, source_target_pairs={{0,1},{1,0},{2,3},{3,2},{4,5},{5,4},{6,7},{7,6},{8,9},{9,8},{10,11... | collective-permute-start | bytes 393224 | tf_op jit(solution)/shard_map/ppermute | solution.py:189
  24.9 1.6 %collective-permute-start.10 = (f32[4,136,128]{2,1,0:T(8,128)S(1)}, f32[4,136,128]{2,1,0:T(8,128)S(1)}, u32[]{:S(2)}, u32[]{:S(2)}) collective-permute-start(f32[4,136,128]{2,1,0:T(8,128)S(1)} %slice.62), channel_id=1, source_target_pairs={{0,1},{1,0},{2,3},{3,2},{4,5},{5,4},{6,7},{7,6},{8,9},{9,8},{10,11... | collective-permute-start | bytes 835592 | tf_op jit(solution)/shard_map/ppermute | solution.py:189
  26.6 5.8 %collective-permute-start.11 = (f32[2,136,128]{2,1,0:T(8,128)S(1)}, f32[2,136,128]{2,1,0:T(8,128)S(1)}, u32[]{:S(2)}, u32[]{:S(2)}) collective-permute-start(f32[2,136,128]{2,1,0:T(8,128)S(1)} %slice.75), channel_id=1, source_target_pairs={{0,2},{1,3},{2,0},{3,1},{4,6},{5,7},{6,4},{7,5},{8,10},{9,11},{10,... | collective-permute-start | bytes 417800 | tf_op jit(solution)/shard_map/ppermute | solution.py:189
  32.5 4.4 %collective-permute-start.12 = (f32[1,136,128]{2,1,0:T(8,128)S(1)}, f32[1,136,128]{2,1,0:T(8,128)S(1)}, u32[]{:S(2)}, u32[]{:S(2)}) collective-permute-start(f32[1,136,128]{2,1,0:T(8,128)S(1)} %slice.77), channel_id=1, source_target_pairs={{0,16},{16,0},{1,17},{17,1},{2,18},{18,2},{3,19},{19,3},{4,20},{20... | collective-permute-start | bytes 208904 | tf_op jit(solution)/shard_map/ppermute | solution.py:189
  36.6 1.9 %collective-permute-start.5 = (f32[8,8,512]{2,1,0:T(8,128)S(1)}, f32[8,8,512]{2,1,0:T(8,128)S(1)}, u32[]{:S(2)}, u32[]{:S(2)}) collective-permute-start(f32[8,8,512]{2,1,0:T(8,128)S(1)} %slice.52), channel_id=1, source_target_pairs={{0,1},{1,0},{2,3},{3,2},{4,5},{5,4},{6,7},{7,6},{8,9},{9,8},{10,11... | collective-permute-start | bytes 393224 | tf_op jit(solution)/shard_map/ppermute | solution.py:189
  36.8 4.5 %collective-permute-start.13 = (f32[1,136,128]{2,1,0:T(8,128)S(1)}, f32[1,136,128]{2,1,0:T(8,128)S(1)}, u32[]{:S(2)}, u32[]{:S(2)}) collective-permute-start(f32[1,136,128]{2,1,0:T(8,128)S(1)} %slice_add_fusion.3), channel_id=1, source_target_pairs={{0,4},{1,5},{2,6},{3,7},{4,0},{5,1},{6,2},{7,3},{8,12},{9,13},{10,... | collective-permute-start | bytes 208904 | tf_op jit(solution)/shard_map/ppermute | solution.py:189
  38.5 4.3 %collective-permute-start.6 = (f32[4,8,512]{2,1,0:T(8,128)S(1)}, f32[4,8,512]{2,1,0:T(8,128)S(1)}, u32[]{:S(2)}, u32[]{:S(2)}) collective-permute-start(f32[4,8,512]{2,1,0:T(8,128)S(1)} %slice.69), channel_id=1, source_target_pairs={{0,2},{1,3},{2,0},{3,1},{4,6},{5,7},{6,4},{7,5},{8,10},{9,11},{10,... | collective-permute-start | bytes 196616 | tf_op jit(solution)/shard_map/ppermute | solution.py:189
  41.3 7.3 %collective-permute-start.14 = (f32[1,136,128]{2,1,0:T(8,128)S(1)}, f32[1,136,128]{2,1,0:T(8,128)S(1)}, u32[]{:S(2)}, u32[]{:S(2)}) collective-permute-start(f32[1,136,128]{2,1,0:T(8,128)S(1)} %add.38), channel_id=1, source_target_pairs={{0,8},{1,9},{2,10},{3,11},{4,12},{5,13},{6,14},{7,15},{8,0},{9,1},... | collective-permute-start | bytes 208904 | tf_op jit(solution)/shard_map/ppermute | solution.py:189
  42.9 6.1 %collective-permute-start.7 = (f32[2,8,512]{2,1,0:T(8,128)S(1)}, f32[2,8,512]{2,1,0:T(8,128)S(1)}, u32[]{:S(2)}, u32[]{:S(2)}) collective-permute-start(f32[2,8,512]{2,1,0:T(8,128)S(1)} %slice.71), channel_id=1, source_target_pairs={{0,8},{1,9},{2,10},{3,11},{4,12},{5,13},{6,14},{7,15},{8,0},{9,1},... | collective-permute-start | bytes 98312 | tf_op jit(solution)/shard_map/ppermute | solution.py:189
  44.4 19.5 %collective-permute-start.9 = (f32[1,32,4096]{2,1,0:T(8,128)S(1)}, f32[1,32,4096]{2,1,0:T(8,128)S(1)}, u32[]{:S(2)}, u32[]{:S(2)}) collective-permute-start(f32[1,32,4096]{2,1,0:T(8,128)S(1)} %slice.60), channel_id=1, source_target_pairs={{0,16},{16,0},{1,17},{17,1},{2,18},{18,2},{3,19},{19,3},{4,20},{20... | collective-permute-start | bytes 1572872 | tf_op jit(solution)/shard_map/ppermute | solution.py:189
  48.6 10.1 %collective-permute-start.15 = (f32[1,136,128]{2,1,0:T(8,128)S(1)}, f32[1,136,128]{2,1,0:T(8,128)S(1)}, u32[]{:S(2)}, u32[]{:S(2)}) collective-permute-start(f32[1,136,128]{2,1,0:T(8,128)S(1)} %add.39), channel_id=1, source_target_pairs={{0,16},{16,0},{1,17},{17,1},{2,18},{18,2},{3,19},{19,3},{4,20},{20... | collective-permute-start | bytes 208904 | tf_op jit(solution)/shard_map/ppermute | solution.py:189
  49.0 11.3 %collective-permute-start.8 = (f32[1,8,512]{2,1,0:T(8,128)S(1)}, f32[1,8,512]{2,1,0:T(8,128)S(1)}, u32[]{:S(2)}, u32[]{:S(2)}) collective-permute-start(f32[1,8,512]{2,1,0:T(8,128)S(1)} %slice.73), channel_id=1, source_target_pairs={{0,4},{1,5},{2,6},{3,7},{4,0},{5,1},{6,2},{7,3},{8,12},{9,13},{10,... | collective-permute-start | bytes 49160 | tf_op jit(solution)/shard_map/ppermute | solution.py:189
  58.8 5.1 %collective-permute-start.16 = (f32[2,136,128]{2,1,0:T(8,128)S(1)}, f32[2,136,128]{2,1,0:T(8,128)S(1)}, u32[]{:S(2)}, u32[]{:S(2)}) collective-permute-start(f32[2,136,128]{2,1,0:T(8,128)S(1)} %pad_maximum_fusion.1), channel_id=1, source_target_pairs={{0,2},{1,3},{2,0},{3,1},{4,6},{5,7},{6,4},{7,5},{8,10},{9,11},{10,... | collective-permute-start | bytes 417800 | tf_op jit(solution)/shard_map/ppermute | solution.py:189
  63.9 1.6 %collective-permute-start.17 = (f32[4,136,128]{2,1,0:T(8,128)S(1)}, f32[4,136,128]{2,1,0:T(8,128)S(1)}, u32[]{:S(2)}, u32[]{:S(2)}) collective-permute-start(f32[4,136,128]{2,1,0:T(8,128)S(1)} %pad_maximum_fusion.refs_0_), channel_id=1, source_target_pairs={{0,1},{1,0},{2,3},{3,2},{4,5},{5,4},{6,7},{7,6},{8,9},{9,8},{10,11... | collective-permute-start | bytes 835592 | tf_op jit(solution)/shard_map/ppermute | solution.py:189

commit v2 on v1

--- a/solution.py
+++ b/solution.py
@@ -6,6 +6,7 @@
 from jax.experimental import pallas as pl
 from jax.experimental.pallas import tpu as pltpu
 from jax.sharding import PartitionSpec as P
+
 
 LANES = 128
 NT = (((1,), (1,)), ((), ()))
@@ -51,7 +52,7 @@
 
 
 class Dims:
-    def __init__(self, mesh, side_a, side_b, pair_grad, out_weight):
+    def __init__(self, mesh, side_a, pair_grad, out_weight):
         self.R, self.Q = mesh.shape["row"], mesh.shape["col"]
         self.rows, self.cols, self.K = pair_grad.shape
         self.CE = out_weight.shape[0]
@@ -68,13 +69,26 @@
         self.JE = self.cols * self.C
 
 
-def first_kernel(d, pg_ref, w_ref, b_ref, gh_ref, gl_ref, bh_ref, bl_ref, t_ref, tb_ref):
-    pg = split(pg_ref[...].reshape(d.rows * d.cols, d.K))
+def fetch(src_ref, dst_ref, sem):
+    copy = pltpu.make_async_copy(src_ref, dst_ref, sem)
+    copy.start()
+    return copy
+
+
+def grad_outer_kernel(d, pg_ref, w_ref, gh_ref, gl_ref, ph_ref, pl_ref, bias_ref, t_ref, pv_ref, wv_ref, sems):
+    w_copy = fetch(w_ref, wv_ref, sems.at[0])
+    p_copy = fetch(pg_ref, pv_ref, sems.at[1])
     pairs = d.rows * d.cols
+    p_copy.wait()
+    flat = pv_ref[...].reshape(pairs, d.K)
+    pg = split(flat)
+    ph_ref[...], pl_ref[...] = split(flat.T)
+    bias_ref[...] = jnp.broadcast_to(jnp.sum(flat, axis=0, keepdims=True), (8, d.K))
+    w_copy.wait()
     two = 2 if d.G % 2 == 0 else 1
     for u in range(0, d.G, two):
         w = jnp.concatenate(
-            [w_ref[pl.ds((p4 * d.G + v) * d.C, d.C), :] for v in range(u, u + two) for p4 in range(d.n)], axis=0
+            [wv_ref[pl.ds((p4 * d.G + v) * d.C, d.C), :] for v in range(u, u + two) for p4 in range(d.n)], axis=0
         )
         out = dot3(pg, split(w), NT)
         for v in range(two):
@@ -90,12 +104,24 @@
         return carry
 
     lax.fori_loop(0, d.rows, body, 0)
-    to_seq(d, b_ref, bh_ref, bl_ref, 0, tb_ref)
+
+
+def own_right_kernel(d, b_ref, bh_ref, bl_ref, tb_ref, sem):
+    copies = [
+        fetch(b_ref.at[:, pl.ds(v * LANES, LANES)], tb_ref.at[pl.ds(v * d.cols, d.cols)], sem) for v in range(d.g)
+    ]
+    for copy in copies:
+        copy.wait()
+    swap_to_seq(d, bh_ref, bl_ref, 0, tb_ref)
 
 
 def to_seq(d, b_ref, bh_ref, bl_ref, at, tb_ref):
     for v in range(d.g):
         tb_ref[pl.ds(v * d.cols, d.cols), :] = b_ref[:, v * LANES:(v + 1) * LANES]
+    swap_to_seq(d, bh_ref, bl_ref, at, tb_ref)
+
+
+def swap_to_seq(d, bh_ref, bl_ref, at, tb_ref):
     for quad in range(d.cols // d.n):
         parts = [tb_ref[pl.ds(quad * d.n + t, d.g, stride=d.cols), :] for t in range(d.n)]
         hi, lo = split(jnp.concatenate(swap_blocks(parts), axis=0))
@@ -103,7 +129,7 @@
         bl_ref[at:at + d.slab, quad * LANES:(quad + 1) * LANES] = lo
 
 
-def second_kernel(d, order, blocks, pg_ref, a_ref, bx_ref, bh_ref, bl_ref, w_ref, ah_ref, al_ref, xh_ref, xl_ref,
+def weight_kernel(d, order, blocks, ph_ref, pl_ref, bias_ref, a_ref, bx_ref, bh_ref, bl_ref, w_ref, ah_ref, al_ref, xh_ref, xl_ref,
                   t_ref, tb_ref, ta_ref, o_ref):
     r, q = lax.axis_index("row"), lax.axis_index("col")
     pairs = d.rows * d.cols
@@ -135,8 +161,7 @@
         return carry
 
     lax.fori_loop(0, d.rows, body, 0)
-    flat = pg_ref[...].reshape(pairs, d.K)
-    turned = split(flat.T)
+    turned = ph_ref[...], pl_ref[...]
     beta = blocks.mine()
     per = d.CE // blocks.count
     for u in range(d.G):
@@ -144,23 +169,26 @@
         for p4 in range(d.n):
             row = (p4 * d.G + u) * d.C
             w_ref[(row // per) ^ beta, pl.ds(row % per, d.C), :] = part[p4 * d.C:(p4 + 1) * d.C]
-    bias = jnp.broadcast_to(jnp.sum(flat, axis=0, keepdims=True), (8, d.K))
     for t in range(blocks.count):
-        w_ref[t, pl.ds(per, 8), :] = bias
-
-
-def third_kernel(d, order, gh_ref, gl_ref, ah_ref, al_ref, xh_ref, xl_ref, gb_ref, ga_ref, tb_ref, ta_ref, o_ref):
-    r, q = lax.axis_index("row"), lax.axis_index("col")
+        w_ref[t, pl.ds(per, 8), :] = bias_ref[...]
+
+
+def right_grad_kernel(d, gh_ref, gl_ref, ah_ref, al_ref, gb_ref, tb_ref, o_ref):
     gt = gh_ref[...], gl_ref[...]
     for m in range(d.R):
         at = slice(m * d.slab, (m + 1) * d.slab)
-        o_ref[0:d.slab, :] = dot3((ah_ref[at, :], al_ref[at, :]), gt, NN)
+        o_ref[...] = dot3((ah_ref[at, :], al_ref[at, :]), gt, NN)
         for quad in range(d.cols // d.n):
             parts = [o_ref[p * d.g:(p + 1) * d.g, quad * LANES:(quad + 1) * LANES] for p in range(d.n)]
             for t, x in enumerate(swap_blocks(parts)):
                 tb_ref[pl.ds(quad * d.n + t, d.g, stride=d.cols), :] = x
         for v in range(d.g):
             gb_ref[m, :, v * LANES:(v + 1) * LANES] = tb_ref[pl.ds(v * d.cols, d.cols), :]
+
+
+def left_grad_kernel(d, order, gh_ref, gl_ref, xh_ref, xl_ref, ga_ref, ta_ref):
+    r, q = lax.axis_index("row"), lax.axis_index("col")
+    gt = gh_ref[...], gl_ref[...]
     for m in range(d.R):
         at = slice(m * d.slab, (m + 1) * d.slab)
         out = dot3((xh_ref[at, :], xl_ref[at, :]), gt, NT) * (1.0 / d.S)
@@ -182,7 +210,7 @@
         w_ref[pl.ds(at, per), :] = mine_ref[t, 0:per, :]
         at = pl.multiple_of(((t + half) ^ beta) * per, per)
         w_ref[pl.ds(at, per), :] = other_ref[t, 0:per, :]
-    bias_ref[...] = mine_ref[0, per:per + 8, :]
+    bias_ref[...] = mine_ref[0, per, :]
 
 
 def swap_with(x, axis, bit, size):
@@ -201,79 +229,107 @@
         return p
 
 
-def call(kernel, outs, scratch, *args):
+VMEM, HBM = pltpu.MemorySpace.VMEM, pltpu.MemorySpace.HBM
+
+
+def call(kernel, outs, scratch, *args, space=VMEM):
     return pl.pallas_call(
         kernel,
         out_shape=outs,
-        scratch_shapes=[pltpu.VMEM(s, jnp.float32) for s in scratch],
+        in_specs=[pl.BlockSpec(memory_space=space)] * len(args),
+        scratch_shapes=[pltpu.VMEM(s, jnp.float32) if isinstance(s, tuple) else s for s in scratch],
         compiler_params=pltpu.CompilerParams(vmem_limit_bytes=48 << 20),
     )(*args)
 
 
+def hbm(x):
+    return pltpu.with_memory_space_constraint(x, HBM)
+
+
 def shape(*dims, dtype=jnp.float32):
     return jax.ShapeDtypeStruct(dims, dtype)
 
 
+def counts(mesh):
+    return {axis: n.bit_length() - 1 for axis, n in mesh.shape.items()}
+
+
 def build(mesh):
-    size = {"row": mesh.shape["row"], "col": mesh.shape["col"]}
-    count = {axis: n.bit_length() - 1 for axis, n in size.items()}
+    size, count = mesh.shape, counts(mesh)
     order = list(range(2, count["col"])) + [b for b in (1, 0) if b < count["col"]]
 
+    def swap(x, axis, bit):
+        return swap_with(x, axis, bit, size[axis])
+
+    def halve(x, axis, bit):
+        n = x.shape[0] // 2
+        send = x[n:]
+        other = swap(send, axis, bit)
+        return x[:n] + other
+
+    def double(x, axis, bit):
+        other = swap(x, axis, bit)
+        return jnp.concatenate([x, other])
+
     def local(side_a, side_b, pair_grad, out_weight):
-        d = Dims(mesh, side_a, side_b, pair_grad, out_weight)
-        half = jnp.bfloat16
-        taken = [("col", 0), ("col", 1), ("row", 0)]
-        rest = [(x, b) for x in ("col", "row") for b in range(count[x]) if (x, b) not in taken]
+        d = Dims(mesh, side_a, pair_grad, out_weight)
+        low = jnp.bfloat16
+        taken, rest = plan(count)
         blocks = Blocks(taken)
         pairs = d.rows * d.cols
         t_s, tb_s, ta_s = (d.G * pairs, LANES), (d.g * d.cols, LANES), (d.g * d.rows, LANES)
-        o_s = (max(d.S, d.IC), d.JE)
-
+        dma = pltpu.SemaphoreType.DMA
+
+        left = side_a[None]
+        for bit in order:
+            left = double(left, "col", bit)
         right = side_b[None]
         for bit in range(count["row"]):
-            right = jnp.concatenate([right, swap_with(right, "row", bit, d.R)])
-        left = side_a[None]
-        for bit in order:
-            left = jnp.concatenate([left, swap_with(left, "col", bit, d.Q)])
-
-        big, small = shape(d.IC, d.JE, dtype=half), shape(d.slab, d.JE, dtype=half)
-        gh, gl, bh, bl = call(
-            lambda *refs: first_kernel(d, *refs), [big, big, small, small], [t_s, tb_s], pair_grad, out_weight, side_b
-        )
-        amat, bmat = shape(d.S, d.IC, dtype=half), shape(d.S, d.JE, dtype=half)
+            right = double(right, "row", bit)
+
+        big, small, turn = shape(d.IC, d.JE, dtype=low), shape(d.slab, d.JE, dtype=low), shape(d.K, pairs, dtype=low)
+        gh, gl, ph, plo, bias = call(
+            lambda *refs: grad_outer_kernel(d, *refs), [big, big, turn, turn, shape(8, d.K)],
+            [t_s, (d.rows, d.cols, d.K), (d.CE, d.K), dma((2,))], hbm(pair_grad), hbm(out_weight), space=HBM,
+        )
+        bh, bl = call(lambda *refs: own_right_kernel(d, *refs), [small, small], [tb_s, dma(())], hbm(side_b), space=HBM)
+        amat, bmat = shape(d.S, d.IC, dtype=low), shape(d.S, d.JE, dtype=low)
         per = d.CE // blocks.count
         part, ah, al, xh, xl = call(
-            lambda *refs: second_kernel(d, order, blocks, *refs),
+            lambda *refs: weight_kernel(d, order, blocks, *refs),
             [shape(blocks.count, per + 8, d.K), amat, amat, bmat, bmat],
-            [t_s, tb_s, ta_s, o_s],
-            pair_grad, left, right[1:], bh, bl,
-        )
-        gb, ga = call(
-            lambda *refs: third_kernel(d, order, *refs),
-            [shape(d.R, d.cols, d.slab * d.C), shape(d.Q, d.rows, d.blk)],
-            [tb_s, ta_s, (d.slab, d.JE)],
-            gh, gl, ah, al, xh, xl,
-        )
+            [t_s, tb_s, ta_s, (max(d.S, d.IC), d.JE)],
+            ph, plo, bias, left, right[1:], bh, bl,
+        )
+        gb = call(
+            lambda *refs: right_grad_kernel(d, *refs), shape(d.R, d.cols, d.slab * d.C),
+            [tb_s, (d.slab, d.JE)], gh, gl, ah, al,
+        )
+        ga = call(lambda *refs: left_grad_kernel(d, order, *refs), shape(d.Q, d.rows, d.blk), [ta_s], gh, gl, xh, xl)
         for axis, bit in taken:
-            n = part.shape[0] // 2
-            part = part[:n] + swap_with(part[n:], axis, bit, size[axis])
+            part = halve(part, axis, bit)
         for axis, bit in rest:
-            part = part + swap_with(part, axis, bit, size[axis])
+            other = swap(part, axis, bit)
+            part = part + other
         for axis, bit in taken[:0:-1]:
-            part = jnp.concatenate([part, swap_with(part, axis, bit, size[axis])])
-        other = swap_with(part, *taken[0], size[taken[0][0]])
+            part = double(part, axis, bit)
+        other = swap(part, *taken[0])
         weight, bias = call(
-            lambda *refs: last_kernel(blocks, per, *refs), [shape(d.CE, d.K), shape(8, d.K)], [], part, other
-        )
-        for bit in range(count["row"] - 1, -1, -1):
-            n = gb.shape[0] // 2
-            gb = gb[:n] + swap_with(gb[n:], "row", bit, d.R)
+            lambda *refs: last_kernel(blocks, per, *refs), [shape(d.CE, d.K), shape(d.K)], [], part, other
+        )
+        for bit in reversed(range(count["row"])):
+            gb = halve(gb, "row", bit)
         for bit in order[::-1]:
-            n = ga.shape[0] // 2
-            ga = ga[:n] + swap_with(ga[n:], "col", bit, d.Q)
-        return ga[0], gb[0], weight, bias[0]
+            ga = halve(ga, "col", bit)
+        return ga[0], gb[0], weight, bias
 
     return local
+
+
+def plan(count):
+    taken = [("col", b) for b in range(min(3, count["col"]))]
+    rest = [("col", b) for b in range(3, count["col"])] + [("row", b) for b in range(count["row"])]
+    return taken, rest
 
 
 def solution(mesh):

time: 67.2 us -> 59 us (0.88)
  waiting for transfers between devices: 27.7 us -> 19.7 us
  local copies, waits for them, and re-layouts: 3.63 us -> 0.13 us
  Pallas kernels: 10 us -> 12.7 us
  starting transfers between devices: 22.4 us -> 23.1 us
    ppermute x18, waiting for transfers between devices: 27.7 us -> 19.7 us  [swap_with(): return lax.ppermute(x, axis, [(i, i ^ 1 << bit) for i in range(size)])]
    unnamed x12 -> x6, local copies, waits for them, and re-layouts: 3.01 us -> 0.02 us
    pallas_call x4 -> x6, Pallas kernels: 10 us -> 12.7 us  [call(): pl.pallas_call(kernel, out_shape=outs, in_specs=[pl.BlockSpec(memory_spac...]
    ppermute x18, starting transfers between devices: 22.4 us -> 23.1 us  [swap_with(): return lax.ppermute(x, axis, [(i, i ^ 1 << bit) for i in range(size)])]
  transfers between devices with their start and end apart: 18 -> 18, of which waited for: 13 -> 10; matrix products, arithmetic and copies ran while one was open for 4% -> 4% of each run, Pallas kernels for 8% -> 14%
where the time goes in v2:
time: 59 us; the launch traced here: 58.8 us
  starting transfers between devices  23.1 us (39%)
  waiting for transfers between devices  19.7 us (33%)
  Pallas kernels  12.7 us (22%)
  other arithmetic  2.37 us (4%)
  between operations  0.84 us (1%)
    ppermute x18, starting transfers between devices, swap_with(): return lax.ppermute(x, axis, [(i, i ^ 1 << bit) for i in range(size)])  23.1 us
    ppermute x18, waiting for transfers between devices, swap_with(): return lax.ppermute(x, axis, [(i, i ^ 1 << bit) for i in range(size)])  19.7 us
    pallas_call x6, Pallas kernels, call(): pl.pallas_call(kernel, out_shape=outs, in_specs=[pl.BlockSpec(memory_spac...  12.7 us
    squeeze x2, other arithmetic, local(): return (ga[0], gb[0], weight, bias)  1.49 us
  transfers between devices with their start and end apart: 18, of which 10 were waited for; matrix products, arithmetic and copies ran while one was open for 4% of the time, Pallas kernels for 14%

profile of v2, /device:TPU:0, one launch (start us, length us, event | category | flops | bytes accessed | tf_op | source)
XLA Modules:
  0.0 58.8 jit_solution(14273576171235245097)
XLA Ops:
  0.6 3.1 %collective-permute-start = (f32[1,8,512]{2,1,0:T(8,128)}, f32[1,8,512]{2,1,0:T(8,128)S(1)}, u32[]{:S(2)}, u32[]{:S(2)}) collective-permute-start(f32[1,8,512]{2,1,0:T(8,128)} %bitcast.8), channel_id=1, source_target_pairs={{0,4},{1,5},{2,6},{3,7},{4,0},{5,1},{6,2},{7,3},{8,12},{9,13},{10,... | collective-permute-start | bytes 49160 | tf_op jit(solution)/shard_map/ppermute | solution.py:217
  3.7 1.5 %collective-permute-start.4 = (f32[1,32,4096]{2,1,0:T(8,128)}, f32[1,32,4096]{2,1,0:T(8,128)S(1)}, u32[]{:S(2)}, u32[]{:S(2)}) collective-permute-start(f32[1,32,4096]{2,1,0:T(8,128)} %bitcast.7), channel_id=1, source_target_pairs={{0,16},{16,0},{1,17},{17,1},{2,18},{18,2},{3,19},{19,3},{4,20},{20... | collective-permute-start | bytes 1572872 | tf_op jit(solution)/shard_map/ppermute | solution.py:217
  6.4 3.0 %collective-permute-start.1 = (f32[2,8,512]{2,1,0:T(8,128)S(1)}, f32[2,8,512]{2,1,0:T(8,128)S(1)}, u32[]{:S(2)}, u32[]{:S(2)}) collective-permute-start(f32[2,8,512]{2,1,0:T(8,128)S(1)} %pad_maximum_fusion.4), channel_id=1, source_target_pairs={{0,8},{1,9},{2,10},{3,11},{4,12},{5,13},{6,14},{7,15},{8,0},{9,1},... | collective-permute-start | bytes 98312 | tf_op jit(solution)/shard_map/ppermute | solution.py:217
  9.4 1.7 %shard_map.76 = (bf16[128,1024]{1,0:T(8,128)(2,1)S(1)}, bf16[128,1024]{1,0:T(8,128)(2,1)S(1)}) custom-call(f32[32,4096]{1,0:T(8,128)} %refs_0_.3), custom_call_target="tpu_custom_call" | custom-call | tf_op jit(solution)/shard_map/pallas_call | solution.py:236
  11.2 3.5 %shard_map.75 = (bf16[256,1024]{1,0:T(8,128)(2,1)S(1)}, bf16[256,1024]{1,0:T(8,128)(2,1)S(1)}, bf16[128,256]{1,0:T(8,128)(2,1)S(1)}, bf16[128,256]{1,0:T(8,128)(2,1)S(1)}, f32[8,128]{1,0:T(8,128)S(1)}) custom-call(f32[8,32,128]{2,1,0:T(8,128)} %refs_0_.2, f32[1024,128]{1,0:T(8,128)} %refs_1_.1), custom_call_target="tpu_custom_call" | custom-call | tf_op jit(solution)/shard_map/pallas_call | solution.py:236
  14.7 1.6 %collective-permute-start.2 = (f32[4,8,512]{2,1,0:T(8,128)S(1)}, f32[4,8,512]{2,1,0:T(8,128)S(1)}, u32[]{:S(2)}, u32[]{:S(2)}) collective-permute-start(f32[4,8,512]{2,1,0:T(8,128)S(1)} %pad_maximum_fusion.3), channel_id=1, source_target_pairs={{0,2},{1,3},{2,0},{3,1},{4,6},{5,7},{6,4},{7,5},{8,10},{9,11},{10,... | collective-permute-start | bytes 196616 | tf_op jit(solution)/shard_map/ppermute | solution.py:217
  16.2 2.8 %collective-permute-done.2 = f32[4,8,512]{2,1,0:T(8,128)S(1)} collective-permute-done((f32[4,8,512]{2,1,0:T(8,128)S(1)}, f32[4,8,512]{2,1,0:T(8,128)S(1)}, u32[]{:S(2)}, u32[]{:S(2)}) %collective-permute-start.2) | collective-permute-done | bytes 65568 | tf_op jit(solution)/shard_map/ppermute | solution.py:217
  19.1 1.3 %collective-permute-done.3 = f32[8,8,512]{2,1,0:T(8,128)S(1)} collective-permute-done((f32[8,8,512]{2,1,0:T(8,128)S(1)}, f32[8,8,512]{2,1,0:T(8,128)S(1)}, u32[]{:S(2)}, u32[]{:S(2)}) %collective-permute-start.3) | collective-permute-done | bytes 131104 | tf_op jit(solution)/shard_map/ppermute | solution.py:217
  20.4 3.6 %shard_map.77 = (f32[8,136,128]{2,1,0:T(8,128)S(1)}, bf16[256,256]{1,0:T(8,128)(2,1)S(1)}, bf16[256,256]{1,0:T(8,128)(2,1)S(1)}, bf16[256,1024]{1,0:T(8,128)(2,1)S(1)}, bf16[256,1024]{1,0:T(8,128)(2,1)S(1)}) custom-call(bf16[128,256]{1,0:T(8,128)(2,1)S(1)} %get-tuple-element.20.refs_0_, bf16[128,256]{1,0:T(8,128)(2,1)S(1)} %get-tuple-element.21.refs_1_, ...), custom_call_target="tpu_custom_call" | custom-call | tf_op jit(solution)/shard_map/pallas_call | solution.py:236
  24.3 1.4 %collective-permute-done.10 = f32[4,136,128]{2,1,0:T(8,128)S(1)} collective-permute-done((f32[4,136,128]{2,1,0:T(8,128)S(1)}, f32[4,136,128]{2,1,0:T(8,128)S(1)}, u32[]{:S(2)}, u32[]{:S(2)}) %collective-permute-start.10) | collective-permute-done | bytes 278560 | tf_op jit(solution)/shard_map/ppermute | solution.py:217
  25.8 1.6 %collective-permute-start.11 = (f32[2,136,128]{2,1,0:T(8,128)S(1)}, f32[2,136,128]{2,1,0:T(8,128)S(1)}, u32[]{:S(2)}, u32[]{:S(2)}) collective-permute-start(f32[2,136,128]{2,1,0:T(8,128)S(1)} %slice.75), channel_id=1, source_target_pairs={{0,2},{1,3},{2,0},{3,1},{4,6},{5,7},{6,4},{7,5},{8,10},{9,11},{10,... | collective-permute-start | bytes 417800 | tf_op jit(solution)/shard_map/ppermute | solution.py:217
  27.3 4.2 %collective-permute-done.11 = f32[2,136,128]{2,1,0:T(8,128)S(1)} collective-permute-done((f32[2,136,128]{2,1,0:T(8,128)S(1)}, f32[2,136,128]{2,1,0:T(8,128)S(1)}, u32[]{:S(2)}, u32[]{:S(2)}) %collective-permute-start.11) | collective-permute-done | bytes 139296 | tf_op jit(solution)/shard_map/ppermute | solution.py:217
  31.6 1.6 %collective-permute-start.12 = (f32[1,136,128]{2,1,0:T(8,128)S(1)}, f32[1,136,128]{2,1,0:T(8,128)S(1)}, u32[]{:S(2)}, u32[]{:S(2)}) collective-permute-start(f32[1,136,128]{2,1,0:T(8,128)S(1)} %slice.77), channel_id=1, source_target_pairs={{0,4},{1,5},{2,6},{3,7},{4,0},{5,1},{6,2},{7,3},{8,12},{9,13},{10,... | collective-permute-start | bytes 208904 | tf_op jit(solution)/shard_map/ppermute | solution.py:217
  33.3 1.4 %shard_map.78 = f32[16,8,512]{2,1,0:T(8,128)S(1)} custom-call(bf16[256,1024]{1,0:T(8,128)(2,1)S(1)} %get-tuple-element.18.refs_0_, bf16[256,1024]{1,0:T(8,128)(2,1)S(1)} %get-tuple-element.19.refs_1_, bf16[256,1024]{1,0:T(8,128)(2,1)S(1)} %get-tuple-element.25.refs_2_, bf16[256,1024]{1,0:T(8,128)(2,1)S(1)} %get-tuple-element.26.refs_3_), custom_call_target="tpu_custom_call" | custom-call | tf_op jit(solution)/shard_map/pallas_call | solution.py:236
  36.2 1.8 %collective-permute-start.6 = (f32[4,8,512]{2,1,0:T(8,128)S(1)}, f32[4,8,512]{2,1,0:T(8,128)S(1)}, u32[]{:S(2)}, u32[]{:S(2)}) collective-permute-start(f32[4,8,512]{2,1,0:T(8,128)S(1)} %slice.67), channel_id=1, source_target_pairs={{0,2},{1,3},{2,0},{3,1},{4,6},{5,7},{6,4},{7,5},{8,10},{9,11},{10,... | collective-permute-start | bytes 196616 | tf_op jit(solution)/shard_map/ppermute | solution.py:217
  38.0 3.3 %collective-permute-done.13 = f32[1,136,128]{2,1,0:T(8,128)S(1)} collective-permute-done((f32[1,136,128]{2,1,0:T(8,128)S(1)}, f32[1,136,128]{2,1,0:T(8,128)S(1)}, u32[]{:S(2)}, u32[]{:S(2)}) %collective-permute-start.13) | collective-permute-done | bytes 69664 | tf_op jit(solution)/shard_map/ppermute | solution.py:217
  41.3 1.6 %collective-permute-start.14 = (f32[1,136,128]{2,1,0:T(8,128)S(1)}, f32[1,136,128]{2,1,0:T(8,128)S(1)}, u32[]{:S(2)}, u32[]{:S(2)}) collective-permute-start(f32[1,136,128]{2,1,0:T(8,128)S(1)} %add.38), channel_id=1, source_target_pairs={{0,16},{16,0},{1,17},{17,1},{2,18},{18,2},{3,19},{19,3},{4,20},{20... | collective-permute-start | bytes 208904 | tf_op jit(solution)/shard_map/ppermute | solution.py:217
  43.5 1.6 %shard_map.79 = f32[2,32,4096]{2,1,0:T(8,128)S(1)} custom-call(bf16[256,1024]{1,0:T(8,128)(2,1)S(1)} %get-tuple-element.18.refs_0_, bf16[256,1024]{1,0:T(8,128)(2,1)S(1)} %get-tuple-element.19.refs_1_, bf16[256,256]{1,0:T(8,128)(2,1)S(1)} %get-tuple-element.27.refs_2_, bf16[256,256]{1,0:T(8,128)(2,1)S(1)} %get-tuple-element.28.refs_3_), custom_call_target="tpu_custom_call" | custom-call | tf_op jit(solution)/shard_map/pallas_call | solution.py:236
  45.2 1.6 %collective-permute-start.9 = (f32[1,32,4096]{2,1,0:T(8,128)S(1)}, f32[1,32,4096]{2,1,0:T(8,128)S(1)}, u32[]{:S(2)}, u32[]{:S(2)}) collective-permute-start(f32[1,32,4096]{2,1,0:T(8,128)S(1)} %slice.73), channel_id=1, source_target_pairs={{0,16},{16,0},{1,17},{17,1},{2,18},{18,2},{3,19},{19,3},{4,20},{20... | collective-permute-start | bytes 1572872 | tf_op jit(solution)/shard_map/ppermute | solution.py:217
  46.8 1.6 %collective-permute-start.15 = (f32[1,136,128]{2,1,0:T(8,128)S(1)}, f32[1,136,128]{2,1,0:T(8,128)S(1)}, u32[]{:S(2)}, u32[]{:S(2)}) collective-permute-start(f32[1,136,128]{2,1,0:T(8,128)S(1)} %add.39), channel_id=1, source_target_pairs={{0,4},{1,5},{2,6},{3,7},{4,0},{5,1},{6,2},{7,3},{8,12},{9,13},{10,... | collective-permute-start | bytes 208904 | tf_op jit(solution)/shard_map/ppermute | solution.py:217
  48.4 1.4 %collective-permute-start.8 = (f32[1,8,512]{2,1,0:T(8,128)S(1)}, f32[1,8,512]{2,1,0:T(8,128)S(1)}, u32[]{:S(2)}, u32[]{:S(2)}) collective-permute-start(f32[1,8,512]{2,1,0:T(8,128)S(1)} %slice.71), channel_id=1, source_target_pairs={{0,4},{1,5},{2,6},{3,7},{4,0},{5,1},{6,2},{7,3},{8,12},{9,13},{10,... | collective-permute-start | bytes 49160 | tf_op jit(solution)/shard_map/ppermute | solution.py:217
  49.8 1.3 %collective-permute-done.15 = f32[1,136,128]{2,1,0:T(8,128)S(1)} collective-permute-done((f32[1,136,128]{2,1,0:T(8,128)S(1)}, f32[1,136,128]{2,1,0:T(8,128)S(1)}, u32[]{:S(2)}, u32[]{:S(2)}) %collective-permute-start.15) | collective-permute-done | bytes 69664 | tf_op jit(solution)/shard_map/ppermute | solution.py:217
  51.1 1.5 %collective-permute-start.16 = (f32[2,136,128]{2,1,0:T(8,128)S(1)}, f32[2,136,128]{2,1,0:T(8,128)S(1)}, u32[]{:S(2)}, u32[]{:S(2)}) collective-permute-start(f32[2,136,128]{2,1,0:T(8,128)S(1)} %pad_maximum_fusion.1), channel_id=1, source_target_pairs={{0,2},{1,3},{2,0},{3,1},{4,6},{5,7},{6,4},{7,5},{8,10},{9,11},{10,... | collective-permute-start | bytes 417800 | tf_op jit(solution)/shard_map/ppermute | solution.py:217
  53.3 3.0 %collective-permute-done.16 = f32[2,136,128]{2,1,0:T(8,128)S(1)} collective-permute-done((f32[2,136,128]{2,1,0:T(8,128)S(1)}, f32[2,136,128]{2,1,0:T(8,128)S(1)}, u32[]{:S(2)}, u32[]{:S(2)}) %collective-permute-start.16) | collective-permute-done | bytes 139296 | tf_op jit(solution)/shard_map/ppermute | solution.py:217
  (48 shorter events, 6.9 us)
Async XLA Ops:
  0.6 5.0 %collective-permute-start = (f32[1,8,512]{2,1,0:T(8,128)}, f32[1,8,512]{2,1,0:T(8,128)S(1)}, u32[]{:S(2)}, u32[]{:S(2)}) collective-permute-start(f32[1,8,512]{2,1,0:T(8,128)} %bitcast.8), channel_id=1, source_target_pairs={{0,4},{1,5},{2,6},{3,7},{4,0},{5,1},{6,2},{7,3},{8,12},{9,13},{10,... | collective-permute-start | bytes 49160 | tf_op jit(solution)/shard_map/ppermute | solution.py:217
  3.7 5.7 %copy-start = (f32[8,512]{1,0:T(8,128)S(1)}, f32[8,512]{1,0:T(8,128)}, u32[]{:S(2)}) copy-start(f32[8,512]{1,0:T(8,128)} %param.4) | copy-start | bytes 49156
  3.7 16.7 %collective-permute-start.4 = (f32[1,32,4096]{2,1,0:T(8,128)}, f32[1,32,4096]{2,1,0:T(8,128)S(1)}, u32[]{:S(2)}, u32[]{:S(2)}) collective-permute-start(f32[1,32,4096]{2,1,0:T(8,128)} %bitcast.7), channel_id=1, source_target_pairs={{0,16},{16,0},{1,17},{17,1},{2,18},{18,2},{3,19},{19,3},{4,20},{20... | collective-permute-start | bytes 1572872 | tf_op jit(solution)/shard_map/ppermute | solution.py:217
  6.4 8.2 %collective-permute-start.1 = (f32[2,8,512]{2,1,0:T(8,128)S(1)}, f32[2,8,512]{2,1,0:T(8,128)S(1)}, u32[]{:S(2)}, u32[]{:S(2)}) collective-permute-start(f32[2,8,512]{2,1,0:T(8,128)S(1)} %pad_maximum_fusion.4), channel_id=1, source_target_pairs={{0,8},{1,9},{2,10},{3,11},{4,12},{5,13},{6,14},{7,15},{8,0},{9,1},... | collective-permute-start | bytes 98312 | tf_op jit(solution)/shard_map/ppermute | solution.py:217
  14.7 4.3 %collective-permute-start.2 = (f32[4,8,512]{2,1,0:T(8,128)S(1)}, f32[4,8,512]{2,1,0:T(8,128)S(1)}, u32[]{:S(2)}, u32[]{:S(2)}) collective-permute-start(f32[4,8,512]{2,1,0:T(8,128)S(1)} %pad_maximum_fusion.3), channel_id=1, source_target_pairs={{0,2},{1,3},{2,0},{3,1},{4,6},{5,7},{6,4},{7,5},{8,10},{9,11},{10,... | collective-permute-start | bytes 196616 | tf_op jit(solution)/shard_map/ppermute | solution.py:217
  19.0 1.4 %collective-permute-start.3 = (f32[8,8,512]{2,1,0:T(8,128)S(1)}, f32[8,8,512]{2,1,0:T(8,128)S(1)}, u32[]{:S(2)}, u32[]{:S(2)}) collective-permute-start(f32[8,8,512]{2,1,0:T(8,128)S(1)} %pad_maximum_fusion.2), channel_id=1, source_target_pairs={{0,1},{1,0},{2,3},{3,2},{4,5},{5,4},{6,7},{7,6},{8,9},{9,8},{10,11... | collective-permute-start | bytes 393224 | tf_op jit(solution)/shard_map/ppermute | solution.py:217
  24.1 1.6 %collective-permute-start.10 = (f32[4,136,128]{2,1,0:T(8,128)S(1)}, f32[4,136,128]{2,1,0:T(8,128)S(1)}, u32[]{:S(2)}, u32[]{:S(2)}) collective-permute-start(f32[4,136,128]{2,1,0:T(8,128)S(1)} %slice.59), channel_id=1, source_target_pairs={{0,1},{1,0},{2,3},{3,2},{4,5},{5,4},{6,7},{7,6},{8,9},{9,8},{10,11... | collective-permute-start | bytes 835592 | tf_op jit(solution)/shard_map/ppermute | solution.py:217
  25.8 5.8 %collective-permute-start.11 = (f32[2,136,128]{2,1,0:T(8,128)S(1)}, f32[2,136,128]{2,1,0:T(8,128)S(1)}, u32[]{:S(2)}, u32[]{:S(2)}) collective-permute-start(f32[2,136,128]{2,1,0:T(8,128)S(1)} %slice.75), channel_id=1, source_target_pairs={{0,2},{1,3},{2,0},{3,1},{4,6},{5,7},{6,4},{7,5},{8,10},{9,11},{10,... | collective-permute-start | bytes 417800 | tf_op jit(solution)/shard_map/ppermute | solution.py:217
  31.6 4.4 %collective-permute-start.12 = (f32[1,136,128]{2,1,0:T(8,128)S(1)}, f32[1,136,128]{2,1,0:T(8,128)S(1)}, u32[]{:S(2)}, u32[]{:S(2)}) collective-permute-start(f32[1,136,128]{2,1,0:T(8,128)S(1)} %slice.77), channel_id=1, source_target_pairs={{0,4},{1,5},{2,6},{3,7},{4,0},{5,1},{6,2},{7,3},{8,12},{9,13},{10,... | collective-permute-start | bytes 208904 | tf_op jit(solution)/shard_map/ppermute | solution.py:217
  34.6 1.5 %collective-permute-start.5 = (f32[8,8,512]{2,1,0:T(8,128)S(1)}, f32[8,8,512]{2,1,0:T(8,128)S(1)}, u32[]{:S(2)}, u32[]{:S(2)}) collective-permute-start(f32[8,8,512]{2,1,0:T(8,128)S(1)} %slice.65), channel_id=1, source_target_pairs={{0,1},{1,0},{2,3},{3,2},{4,5},{5,4},{6,7},{7,6},{8,9},{9,8},{10,11... | collective-permute-start | bytes 393224 | tf_op jit(solution)/shard_map/ppermute | solution.py:217
  36.0 5.3 %collective-permute-start.13 = (f32[1,136,128]{2,1,0:T(8,128)S(1)}, f32[1,136,128]{2,1,0:T(8,128)S(1)}, u32[]{:S(2)}, u32[]{:S(2)}) collective-permute-start(f32[1,136,128]{2,1,0:T(8,128)S(1)} %slice_add_fusion.4), channel_id=1, source_target_pairs={{0,8},{1,9},{2,10},{3,11},{4,12},{5,13},{6,14},{7,15},{8,0},{9,1},... | collective-permute-start | bytes 208904 | tf_op jit(solution)/shard_map/ppermute | solution.py:217
  36.2 6.7 %collective-permute-start.6 = (f32[4,8,512]{2,1,0:T(8,128)S(1)}, f32[4,8,512]{2,1,0:T(8,128)S(1)}, u32[]{:S(2)}, u32[]{:S(2)}) collective-permute-start(f32[4,8,512]{2,1,0:T(8,128)S(1)} %slice.67), channel_id=1, source_target_pairs={{0,2},{1,3},{2,0},{3,1},{4,6},{5,7},{6,4},{7,5},{8,10},{9,11},{10,... | collective-permute-start | bytes 196616 | tf_op jit(solution)/shard_map/ppermute | solution.py:217
  41.3 5.5 %collective-permute-start.14 = (f32[1,136,128]{2,1,0:T(8,128)S(1)}, f32[1,136,128]{2,1,0:T(8,128)S(1)}, u32[]{:S(2)}, u32[]{:S(2)}) collective-permute-start(f32[1,136,128]{2,1,0:T(8,128)S(1)} %add.38), channel_id=1, source_target_pairs={{0,16},{16,0},{1,17},{17,1},{2,18},{18,2},{3,19},{19,3},{4,20},{20... | collective-permute-start | bytes 208904 | tf_op jit(solution)/shard_map/ppermute | solution.py:217
  42.9 5.5 %collective-permute-start.7 = (f32[2,8,512]{2,1,0:T(8,128)S(1)}, f32[2,8,512]{2,1,0:T(8,128)S(1)}, u32[]{:S(2)}, u32[]{:S(2)}) collective-permute-start(f32[2,8,512]{2,1,0:T(8,128)S(1)} %slice.69), channel_id=1, source_target_pairs={{0,8},{1,9},{2,10},{3,11},{4,12},{5,13},{6,14},{7,15},{8,0},{9,1},... | collective-permute-start | bytes 98312 | tf_op jit(solution)/shard_map/ppermute | solution.py:217
  45.2 11.9 %collective-permute-start.9 = (f32[1,32,4096]{2,1,0:T(8,128)S(1)}, f32[1,32,4096]{2,1,0:T(8,128)S(1)}, u32[]{:S(2)}, u32[]{:S(2)}) collective-permute-start(f32[1,32,4096]{2,1,0:T(8,128)S(1)} %slice.73), channel_id=1, source_target_pairs={{0,16},{16,0},{1,17},{17,1},{2,18},{18,2},{3,19},{19,3},{4,20},{20... | collective-permute-start | bytes 1572872 | tf_op jit(solution)/shard_map/ppermute | solution.py:217
  46.8 4.4 %collective-permute-start.15 = (f32[1,136,128]{2,1,0:T(8,128)S(1)}, f32[1,136,128]{2,1,0:T(8,128)S(1)}, u32[]{:S(2)}, u32[]{:S(2)}) collective-permute-start(f32[1,136,128]{2,1,0:T(8,128)S(1)} %add.39), channel_id=1, source_target_pairs={{0,4},{1,5},{2,6},{3,7},{4,0},{5,1},{6,2},{7,3},{8,12},{9,13},{10,... | collective-permute-start | bytes 208904 | tf_op jit(solution)/shard_map/ppermute | solution.py:217
  48.4 4.3 %collective-permute-start.8 = (f32[1,8,512]{2,1,0:T(8,128)S(1)}, f32[1,8,512]{2,1,0:T(8,128)S(1)}, u32[]{:S(2)}, u32[]{:S(2)}) collective-permute-start(f32[1,8,512]{2,1,0:T(8,128)S(1)} %slice.71), channel_id=1, source_target_pairs={{0,4},{1,5},{2,6},{3,7},{4,0},{5,1},{6,2},{7,3},{8,12},{9,13},{10,... | collective-permute-start | bytes 49160 | tf_op jit(solution)/shard_map/ppermute | solution.py:217
  51.1 5.1 %collective-permute-start.16 = (f32[2,136,128]{2,1,0:T(8,128)S(1)}, f32[2,136,128]{2,1,0:T(8,128)S(1)}, u32[]{:S(2)}, u32[]{:S(2)}) collective-permute-start(f32[2,136,128]{2,1,0:T(8,128)S(1)} %pad_maximum_fusion.1), channel_id=1, source_target_pairs={{0,2},{1,3},{2,0},{3,1},{4,6},{5,7},{6,4},{7,5},{8,10},{9,11},{10,... | collective-permute-start | bytes 417800 | tf_op jit(solution)/shard_map/ppermute | solution.py:217
  56.3 1.6 %collective-permute-start.17 = (f32[4,136,128]{2,1,0:T(8,128)S(1)}, f32[4,136,128]{2,1,0:T(8,128)S(1)}, u32[]{:S(2)}, u32[]{:S(2)}) collective-permute-start(f32[4,136,128]{2,1,0:T(8,128)S(1)} %pad_maximum_fusion.refs_0_), channel_id=1, source_target_pairs={{0,1},{1,0},{2,3},{3,2},{4,5},{5,4},{6,7},{7,6},{8,9},{9,8},{10,11... | collective-permute-start | bytes 835592 | tf_op jit(solution)/shard_map/ppermute | solution.py:217

commit v3 on v2

--- a/solution.py
+++ b/solution.py
@@ -75,7 +75,7 @@
     return copy
 
 
-def grad_outer_kernel(d, pg_ref, w_ref, gh_ref, gl_ref, ph_ref, pl_ref, bias_ref, t_ref, pv_ref, wv_ref, sems):
+def pair_kernel(d, pg_ref, w_ref, t_ref, ph_ref, pl_ref, bias_ref, pv_ref, wv_ref, sems):
     w_copy = fetch(w_ref, wv_ref, sems.at[0])
     p_copy = fetch(pg_ref, pv_ref, sems.at[1])
     pairs = d.rows * d.cols
@@ -94,16 +94,15 @@
         for v in range(two):
             t_ref[pl.ds((u + v) * pairs, pairs), :] = out[:, v * LANES:(v + 1) * LANES]
 
-    def body(i, carry):
+
+def grad_outer_kernel(d, t_ref, gh_ref, gl_ref):
+    pairs = d.rows * d.cols
+    for i in range(d.rows):
         for quad in range(d.cols // d.n):
             parts = [t_ref[pl.ds(i * d.cols + quad * d.n + t, d.G, stride=pairs), :] for t in range(d.n)]
             hi, lo = split(jnp.concatenate(swap_blocks(parts), axis=0))
-            at = pl.multiple_of(i * d.C, d.C)
-            gh_ref[pl.ds(at, d.C), quad * LANES:(quad + 1) * LANES] = hi
-            gl_ref[pl.ds(at, d.C), quad * LANES:(quad + 1) * LANES] = lo
-        return carry
-
-    lax.fori_loop(0, d.rows, body, 0)
+            gh_ref[i * d.C:(i + 1) * d.C, quad * LANES:(quad + 1) * LANES] = hi
+            gl_ref[i * d.C:(i + 1) * d.C, quad * LANES:(quad + 1) * LANES] = lo
 
 
 def own_right_kernel(d, b_ref, bh_ref, bl_ref, tb_ref, sem):
@@ -152,23 +151,20 @@
     al_ref[...] = lo
     o_ref[0:d.IC, :] = dot3(split(a.T), (xh_ref[...], xl_ref[...]), NN)
 
-    def body(i, carry):
+    for i in range(d.rows):
         for quad in range(d.cols // d.n):
-            parts = [o_ref[pl.ds(pl.multiple_of(i * d.C + p4 * d.G, d.G), d.G), quad * LANES:(quad + 1) * LANES]
-                     for p4 in range(d.n)]
+            parts = [o_ref[pl.ds(i * d.C + p4 * d.G, d.G), quad * LANES:(quad + 1) * LANES] for p4 in range(d.n)]
             for t, x in enumerate(swap_blocks(parts)):
                 t_ref[pl.ds(i * d.cols + quad * d.n + t, d.G, stride=pairs), :] = x
-        return carry
-
-    lax.fori_loop(0, d.rows, body, 0)
     turned = ph_ref[...], pl_ref[...]
-    beta = blocks.mine()
+    keys = blocks.key(0), blocks.key(1)
     per = d.CE // blocks.count
     for u in range(d.G):
         part = dot3(turned, split(t_ref[pl.ds(u * pairs, pairs), :]), NN).T
         for p4 in range(d.n):
             row = (p4 * d.G + u) * d.C
-            w_ref[(row // per) ^ beta, pl.ds(row % per, d.C), :] = part[p4 * d.C:(p4 + 1) * d.C]
+            block = row // per
+            w_ref[block ^ keys[2 * block // blocks.count], pl.ds(row % per, d.C), :] = part[p4 * d.C:(p4 + 1) * d.C]
     for t in range(blocks.count):
         w_ref[t, pl.ds(per, 8), :] = bias_ref[...]
 
@@ -203,29 +199,29 @@
 
 
 def last_kernel(blocks, per, mine_ref, other_ref, w_ref, bias_ref):
-    beta = blocks.mine()
     half = blocks.count // 2
-    for t in range(half):
-        at = pl.multiple_of((t ^ beta) * per, per)
-        w_ref[pl.ds(at, per), :] = mine_ref[t, 0:per, :]
-        at = pl.multiple_of(((t + half) ^ beta) * per, per)
-        w_ref[pl.ds(at, per), :] = other_ref[t, 0:per, :]
+    odd = lax.axis_index("col") & 1
+    for ref, top, key in ((mine_ref, 0, blocks.key(odd)), (other_ref, half, blocks.key(1 - odd))):
+        for t in range(half):
+            at = pl.multiple_of(((t + top) ^ key) * per, per)
+            w_ref[pl.ds(at, per), :] = ref[t, 0:per, :]
     bias_ref[...] = mine_ref[0, per, :]
 
 
-def swap_with(x, axis, bit, size):
-    return lax.ppermute(x, axis, [(i, i ^ (1 << bit)) for i in range(size)])
+def swap_with(x, axis, bits, size):
+    return lax.ppermute(x, axis, [(i, i ^ (1 << bits[i & 1])) for i in range(size)])
 
 
 class Blocks:
-    def __init__(self, bits):
-        self.bits = bits
-        self.count = 1 << len(bits)
-
-    def mine(self):
-        p = 0
-        for axis, bit in self.bits:
-            p = (p << 1) | ((lax.axis_index(axis) >> bit) & 1)
+    def __init__(self, steps):
+        self.steps = steps
+        self.count = 1 << len(steps)
+
+    def key(self, odd):
+        q, p = lax.axis_index("col"), 0
+        for step in self.steps:
+            bit = jnp.where(odd, step[1], step[0]) if not isinstance(odd, int) else step[odd]
+            p = (p << 1) | ((q >> bit) & 1)
         return p
 
 
@@ -259,7 +255,7 @@
     order = list(range(2, count["col"])) + [b for b in (1, 0) if b < count["col"]]
 
     def swap(x, axis, bit):
-        return swap_with(x, axis, bit, size[axis])
+        return swap_with(x, axis, bit if isinstance(bit, tuple) else (bit, bit), size[axis])
 
     def halve(x, axis, bit):
         n = x.shape[0] // 2
@@ -275,7 +271,7 @@
         d = Dims(mesh, side_a, pair_grad, out_weight)
         low = jnp.bfloat16
         taken, rest = plan(count)
-        blocks = Blocks(taken)
+        blocks = Blocks([bits for _, bits in taken])
         pairs = d.rows * d.cols
         t_s, tb_s, ta_s = (d.G * pairs, LANES), (d.g * d.cols, LANES), (d.g * d.rows, LANES)
         dma = pltpu.SemaphoreType.DMA
@@ -288,10 +284,11 @@
             right = double(right, "row", bit)
 
         big, small, turn = shape(d.IC, d.JE, dtype=low), shape(d.slab, d.JE, dtype=low), shape(d.K, pairs, dtype=low)
-        gh, gl, ph, plo, bias = call(
-            lambda *refs: grad_outer_kernel(d, *refs), [big, big, turn, turn, shape(8, d.K)],
-            [t_s, (d.rows, d.cols, d.K), (d.CE, d.K), dma((2,))], hbm(pair_grad), hbm(out_weight), space=HBM,
-        )
+        outer, ph, plo, bias = call(
+            lambda *refs: pair_kernel(d, *refs), [shape(*t_s), turn, turn, shape(8, d.K)],
+            [(d.rows, d.cols, d.K), (d.CE, d.K), dma((2,))], hbm(pair_grad), hbm(out_weight), space=HBM,
+        )
+        gh, gl = call(lambda *refs: grad_outer_kernel(d, *refs), [big, big], [], outer)
         bh, bl = call(lambda *refs: own_right_kernel(d, *refs), [small, small], [tb_s, dma(())], hbm(side_b), space=HBM)
         amat, bmat = shape(d.S, d.IC, dtype=low), shape(d.S, d.JE, dtype=low)
         per = d.CE // blocks.count
@@ -327,8 +324,9 @@
 
 
 def plan(count):
-    taken = [("col", b) for b in range(min(3, count["col"]))]
-    rest = [("col", b) for b in range(3, count["col"])] + [("row", b) for b in range(count["row"])]
+    n = min(3, count["col"])
+    taken = [("col", (0, 0))] + [("col", (b, n - b)) for b in range(1, n)]
+    rest = [("col", b) for b in range(n, count["col"])] + [("row", b) for b in range(count["row"])]
     return taken, rest
 
 

time: 59 us -> 61.3 us (1.039)
  waiting for transfers between devices: 19.7 us -> 22.4 us
  starting transfers between devices: 23.1 us -> 21.4 us
  Pallas kernels: 12.7 us -> 13.9 us
    ppermute x18, waiting for transfers between devices: 19.7 us -> 22.4 us  [swap_with(): lax.ppermute(x, axis, [(i, i ^ 1 << bits[i & 1]) for i in range(size)])]
    ppermute x18, starting transfers between devices: 23.1 us -> 21.4 us  [swap_with(): lax.ppermute(x, axis, [(i, i ^ 1 << bits[i & 1]) for i in range(size)])]
    pallas_call x6 -> x7, Pallas kernels: 12.7 us -> 13.9 us  [call(): pl.pallas_call(kernel, out_shape=outs, in_specs=[pl.BlockSpec(memory_spac...]
  transfers between devices with their start and end apart: 18 -> 18, of which waited for: 10 -> 11; matrix products, arithmetic and copies ran while one was open for 4% -> 4% of each run, Pallas kernels for 14% -> 17%
where the time goes in v3:
time: 61.3 us; the launch traced here: 61.1 us
  waiting for transfers between devices  22.4 us (37%)
  starting transfers between devices  21.4 us (35%)
  Pallas kernels  13.9 us (23%)
  other arithmetic  2.38 us (4%)
  between operations  0.86 us (1%)
    ppermute x18, waiting for transfers between devices, swap_with(): lax.ppermute(x, axis, [(i, i ^ 1 << bits[i & 1]) for i in range(size)])  22.4 us
    ppermute x18, starting transfers between devices, swap_with(): lax.ppermute(x, axis, [(i, i ^ 1 << bits[i & 1]) for i in range(size)])  21.4 us
    pallas_call x7, Pallas kernels, call(): pl.pallas_call(kernel, out_shape=outs, in_specs=[pl.BlockSpec(memory_spac...  13.9 us
    squeeze x2, other arithmetic, local(): return (ga[0], gb[0], weight, bias)  1.49 us
  transfers between devices with their start and end apart: 18, of which 11 were waited for; matrix products, arithmetic and copies ran while one was open for 4% of the time, Pallas kernels for 17%

profile of v3, /device:TPU:0, one launch (start us, length us, event | category | flops | bytes accessed | tf_op | source)
XLA Modules:
  0.0 61.1 jit_solution(4909820345027643554)
XLA Ops:
  0.6 3.1 %collective-permute-start = (f32[1,8,512]{2,1,0:T(8,128)}, f32[1,8,512]{2,1,0:T(8,128)S(1)}, u32[]{:S(2)}, u32[]{:S(2)}) collective-permute-start(f32[1,8,512]{2,1,0:T(8,128)} %bitcast.8), channel_id=1, source_target_pairs={{0,4},{1,5},{2,6},{3,7},{4,0},{5,1},{6,2},{7,3},{8,12},{9,13},{10,... | collective-permute-start | bytes 49160 | tf_op jit(solution)/shard_map/ppermute | solution.py:212
  3.7 1.5 %collective-permute-start.4 = (f32[1,32,4096]{2,1,0:T(8,128)}, f32[1,32,4096]{2,1,0:T(8,128)S(1)}, u32[]{:S(2)}, u32[]{:S(2)}) collective-permute-start(f32[1,32,4096]{2,1,0:T(8,128)} %bitcast.7), channel_id=1, source_target_pairs={{0,16},{16,0},{1,17},{17,1},{2,18},{18,2},{3,19},{19,3},{4,20},{20... | collective-permute-start | bytes 1572872 | tf_op jit(solution)/shard_map/ppermute | solution.py:212
  6.4 3.0 %collective-permute-start.1 = (f32[2,8,512]{2,1,0:T(8,128)S(1)}, f32[2,8,512]{2,1,0:T(8,128)S(1)}, u32[]{:S(2)}, u32[]{:S(2)}) collective-permute-start(f32[2,8,512]{2,1,0:T(8,128)S(1)} %pad_maximum_fusion.4), channel_id=1, source_target_pairs={{0,8},{1,9},{2,10},{3,11},{4,12},{5,13},{6,14},{7,15},{8,0},{9,1},... | collective-permute-start | bytes 98312 | tf_op jit(solution)/shard_map/ppermute | solution.py:212
  9.4 1.7 %shard_map.77 = (bf16[128,1024]{1,0:T(8,128)(2,1)S(1)}, bf16[128,1024]{1,0:T(8,128)(2,1)S(1)}) custom-call(f32[32,4096]{1,0:T(8,128)} %refs_0_.3), custom_call_target="tpu_custom_call" | custom-call | tf_op jit(solution)/shard_map/pallas_call | solution.py:232
  11.2 1.8 %shard_map.75 = (f32[2048,128]{1,0:T(8,128)S(1)}, bf16[128,256]{1,0:T(8,128)(2,1)S(1)}, bf16[128,256]{1,0:T(8,128)(2,1)S(1)}, f32[8,128]{1,0:T(8,128)S(1)}) custom-call(f32[8,32,128]{2,1,0:T(8,128)} %refs_0_.2, f32[1024,128]{1,0:T(8,128)} %refs_1_.1), custom_call_target="tpu_custom_call" | custom-call | tf_op jit(solution)/shard_map/pallas_call | solution.py:232
  13.0 1.6 %collective-permute-start.2 = (f32[4,8,512]{2,1,0:T(8,128)S(1)}, f32[4,8,512]{2,1,0:T(8,128)S(1)}, u32[]{:S(2)}, u32[]{:S(2)}) collective-permute-start(f32[4,8,512]{2,1,0:T(8,128)S(1)} %pad_maximum_fusion.3), channel_id=1, source_target_pairs={{0,2},{1,3},{2,0},{3,1},{4,6},{5,7},{6,4},{7,5},{8,10},{9,11},{10,... | collective-permute-start | bytes 196616 | tf_op jit(solution)/shard_map/ppermute | solution.py:212
  14.5 2.8 %collective-permute-done.2 = f32[4,8,512]{2,1,0:T(8,128)S(1)} collective-permute-done((f32[4,8,512]{2,1,0:T(8,128)S(1)}, f32[4,8,512]{2,1,0:T(8,128)S(1)}, u32[]{:S(2)}, u32[]{:S(2)}) %collective-permute-start.2) | collective-permute-done | bytes 65568 | tf_op jit(solution)/shard_map/ppermute | solution.py:212
  18.7 2.8 %shard_map.78 = (f32[8,136,128]{2,1,0:T(8,128)S(1)}, bf16[256,256]{1,0:T(8,128)(2,1)S(1)}, bf16[256,256]{1,0:T(8,128)(2,1)S(1)}, bf16[256,1024]{1,0:T(8,128)(2,1)S(1)}, bf16[256,1024]{1,0:T(8,128)(2,1)S(1)}) custom-call(bf16[128,256]{1,0:T(8,128)(2,1)S(1)} %get-tuple-element.22.refs_0_, bf16[128,256]{1,0:T(8,128)(2,1)S(1)} %get-tuple-element.23.refs_1_, ...), custom_call_target="tpu_custom_call" | custom-call | tf_op jit(solution)/shard_map/pallas_call | solution.py:232
  21.8 1.4 %collective-permute-done.10 = f32[4,136,128]{2,1,0:T(8,128)S(1)} collective-permute-done((f32[4,136,128]{2,1,0:T(8,128)S(1)}, f32[4,136,128]{2,1,0:T(8,128)S(1)}, u32[]{:S(2)}, u32[]{:S(2)}) %collective-permute-start.10) | collective-permute-done | bytes 278560 | tf_op jit(solution)/shard_map/ppermute | solution.py:212
  23.3 1.6 %collective-permute-start.11 = (f32[2,136,128]{2,1,0:T(8,128)S(1)}, f32[2,136,128]{2,1,0:T(8,128)S(1)}, u32[]{:S(2)}, u32[]{:S(2)}) collective-permute-start(f32[2,136,128]{2,1,0:T(8,128)S(1)} %slice.75), channel_id=1, source_target_pairs={{0,2},{1,5},{2,0},{3,7},{4,6},{5,1},{6,4},{7,3},{8,10},{9,13},{10,... | collective-permute-start | bytes 417800 | tf_op jit(solution)/shard_map/ppermute | solution.py:212
  24.9 3.6 %collective-permute-done.11 = f32[2,136,128]{2,1,0:T(8,128)S(1)} collective-permute-done((f32[2,136,128]{2,1,0:T(8,128)S(1)}, f32[2,136,128]{2,1,0:T(8,128)S(1)}, u32[]{:S(2)}, u32[]{:S(2)}) %collective-permute-start.11) | collective-permute-done | bytes 139296 | tf_op jit(solution)/shard_map/ppermute | solution.py:212
  28.5 1.6 %collective-permute-start.12 = (f32[1,136,128]{2,1,0:T(8,128)S(1)}, f32[1,136,128]{2,1,0:T(8,128)S(1)}, u32[]{:S(2)}, u32[]{:S(2)}) collective-permute-start(f32[1,136,128]{2,1,0:T(8,128)S(1)} %slice.77), channel_id=1, source_target_pairs={{0,4},{1,3},{2,6},{3,1},{4,0},{5,7},{6,2},{7,5},{8,12},{9,11},{10,... | collective-permute-start | bytes 208904 | tf_op jit(solution)/shard_map/ppermute | solution.py:212
  30.1 3.8 %shard_map.76 = (bf16[256,1024]{1,0:T(8,128)(2,1)S(1)}, bf16[256,1024]{1,0:T(8,128)(2,1)S(1)}) custom-call(f32[2048,128]{1,0:T(8,128)S(1)} %get-tuple-element.19.refs_0_), custom_call_target="tpu_custom_call" | custom-call | tf_op jit(solution)/shard_map/pallas_call | solution.py:232
  33.9 1.4 %shard_map.79 = f32[16,8,512]{2,1,0:T(8,128)S(1)} custom-call(bf16[256,1024]{1,0:T(8,128)(2,1)S(1)} %get-tuple-element.20.refs_0_, bf16[256,1024]{1,0:T(8,128)(2,1)S(1)} %get-tuple-element.21.refs_1_, bf16[256,1024]{1,0:T(8,128)(2,1)S(1)} %get-tuple-element.27.refs_2_, bf16[256,1024]{1,0:T(8,128)(2,1)S(1)} %get-tuple-element.28.refs_3_), custom_call_target="tpu_custom_call" | custom-call | tf_op jit(solution)/shard_map/pallas_call | solution.py:232
  35.3 1.5 %collective-permute-start.13 = (f32[1,136,128]{2,1,0:T(8,128)S(1)}, f32[1,136,128]{2,1,0:T(8,128)S(1)}, u32[]{:S(2)}, u32[]{:S(2)}) collective-permute-start(f32[1,136,128]{2,1,0:T(8,128)S(1)} %slice_add_fusion.4), channel_id=1, source_target_pairs={{0,8},{1,9},{2,10},{3,11},{4,12},{5,13},{6,14},{7,15},{8,0},{9,1},... | collective-permute-start | bytes 208904 | tf_op jit(solution)/shard_map/ppermute | solution.py:212
  36.9 1.6 %collective-permute-start.6 = (f32[4,8,512]{2,1,0:T(8,128)S(1)}, f32[4,8,512]{2,1,0:T(8,128)S(1)}, u32[]{:S(2)}, u32[]{:S(2)}) collective-permute-start(f32[4,8,512]{2,1,0:T(8,128)S(1)} %slice.67), channel_id=1, source_target_pairs={{0,2},{1,3},{2,0},{3,1},{4,6},{5,7},{6,4},{7,5},{8,10},{9,11},{10,... | collective-permute-start | bytes 196616 | tf_op jit(solution)/shard_map/ppermute | solution.py:212
  38.5 3.8 %collective-permute-done.13 = f32[1,136,128]{2,1,0:T(8,128)S(1)} collective-permute-done((f32[1,136,128]{2,1,0:T(8,128)S(1)}, f32[1,136,128]{2,1,0:T(8,128)S(1)}, u32[]{:S(2)}, u32[]{:S(2)}) %collective-permute-start.13) | collective-permute-done | bytes 69664 | tf_op jit(solution)/shard_map/ppermute | solution.py:212
  42.3 1.6 %collective-permute-start.14 = (f32[1,136,128]{2,1,0:T(8,128)S(1)}, f32[1,136,128]{2,1,0:T(8,128)S(1)}, u32[]{:S(2)}, u32[]{:S(2)}) collective-permute-start(f32[1,136,128]{2,1,0:T(8,128)S(1)} %add.38), channel_id=1, source_target_pairs={{0,16},{16,0},{1,17},{17,1},{2,18},{18,2},{3,19},{19,3},{4,20},{20... | collective-permute-start | bytes 208904 | tf_op jit(solution)/shard_map/ppermute | solution.py:212
  44.1 1.6 %shard_map.80 = f32[2,32,4096]{2,1,0:T(8,128)S(1)} custom-call(bf16[256,1024]{1,0:T(8,128)(2,1)S(1)} %get-tuple-element.20.refs_0_, bf16[256,1024]{1,0:T(8,128)(2,1)S(1)} %get-tuple-element.21.refs_1_, bf16[256,256]{1,0:T(8,128)(2,1)S(1)} %get-tuple-element.29.refs_2_, bf16[256,256]{1,0:T(8,128)(2,1)S(1)} %get-tuple-element.30.refs_3_), custom_call_target="tpu_custom_call" | custom-call | tf_op jit(solution)/shard_map/pallas_call | solution.py:232
  46.7 1.4 %collective-permute-start.15 = (f32[1,136,128]{2,1,0:T(8,128)S(1)}, f32[1,136,128]{2,1,0:T(8,128)S(1)}, u32[]{:S(2)}, u32[]{:S(2)}) collective-permute-start(f32[1,136,128]{2,1,0:T(8,128)S(1)} %add.39), channel_id=1, source_target_pairs={{0,4},{1,3},{2,6},{3,1},{4,0},{5,7},{6,2},{7,5},{8,12},{9,11},{10,... | collective-permute-start | bytes 208904 | tf_op jit(solution)/shard_map/ppermute | solution.py:212
  48.9 2.3 %collective-permute-done.15 = f32[1,136,128]{2,1,0:T(8,128)S(1)} collective-permute-done((f32[1,136,128]{2,1,0:T(8,128)S(1)}, f32[1,136,128]{2,1,0:T(8,128)S(1)}, u32[]{:S(2)}, u32[]{:S(2)}) %collective-permute-start.15) | collective-permute-done | bytes 69664 | tf_op jit(solution)/shard_map/ppermute | solution.py:212
  51.2 1.6 %collective-permute-start.16 = (f32[2,136,128]{2,1,0:T(8,128)S(1)}, f32[2,136,128]{2,1,0:T(8,128)S(1)}, u32[]{:S(2)}, u32[]{:S(2)}) collective-permute-start(f32[2,136,128]{2,1,0:T(8,128)S(1)} %pad_maximum_fusion.1), channel_id=1, source_target_pairs={{0,2},{1,5},{2,0},{3,7},{4,6},{5,1},{6,4},{7,3},{8,10},{9,13},{10,... | collective-permute-start | bytes 417800 | tf_op jit(solution)/shard_map/ppermute | solution.py:212
  53.4 2.9 %collective-permute-done.16 = f32[2,136,128]{2,1,0:T(8,128)S(1)} collective-permute-done((f32[2,136,128]{2,1,0:T(8,128)S(1)}, f32[2,136,128]{2,1,0:T(8,128)S(1)}, u32[]{:S(2)}, u32[]{:S(2)}) %collective-permute-start.16) | collective-permute-done | bytes 139296 | tf_op jit(solution)/shard_map/ppermute | solution.py:212
  56.4 3.0 %collective-permute-done.9 = f32[1,32,4096]{2,1,0:T(8,128)S(1)} collective-permute-done((f32[1,32,4096]{2,1,0:T(8,128)S(1)}, f32[1,32,4096]{2,1,0:T(8,128)S(1)}, u32[]{:S(2)}, u32[]{:S(2)}) %collective-permute-start.9) | collective-permute-done | bytes 524320 | tf_op jit(solution)/shard_map/ppermute | solution.py:212
  (49 shorter events, 7.3 us)
Async XLA Ops:
  0.6 5.0 %collective-permute-start = (f32[1,8,512]{2,1,0:T(8,128)}, f32[1,8,512]{2,1,0:T(8,128)S(1)}, u32[]{:S(2)}, u32[]{:S(2)}) collective-permute-start(f32[1,8,512]{2,1,0:T(8,128)} %bitcast.8), channel_id=1, source_target_pairs={{0,4},{1,5},{2,6},{3,7},{4,0},{5,1},{6,2},{7,3},{8,12},{9,13},{10,... | collective-permute-start | bytes 49160 | tf_op jit(solution)/shard_map/ppermute | solution.py:212
  3.7 5.7 %copy-start = (f32[8,512]{1,0:T(8,128)S(1)}, f32[8,512]{1,0:T(8,128)}, u32[]{:S(2)}) copy-start(f32[8,512]{1,0:T(8,128)} %param.4) | copy-start | bytes 49156
  3.7 15.0 %collective-permute-start.4 = (f32[1,32,4096]{2,1,0:T(8,128)}, f32[1,32,4096]{2,1,0:T(8,128)S(1)}, u32[]{:S(2)}, u32[]{:S(2)}) collective-permute-start(f32[1,32,4096]{2,1,0:T(8,128)} %bitcast.7), channel_id=1, source_target_pairs={{0,16},{16,0},{1,17},{17,1},{2,18},{18,2},{3,19},{19,3},{4,20},{20... | collective-permute-start | bytes 1572872 | tf_op jit(solution)/shard_map/ppermute | solution.py:212
  6.4 6.5 %collective-permute-start.1 = (f32[2,8,512]{2,1,0:T(8,128)S(1)}, f32[2,8,512]{2,1,0:T(8,128)S(1)}, u32[]{:S(2)}, u32[]{:S(2)}) collective-permute-start(f32[2,8,512]{2,1,0:T(8,128)S(1)} %pad_maximum_fusion.4), channel_id=1, source_target_pairs={{0,8},{1,9},{2,10},{3,11},{4,12},{5,13},{6,14},{7,15},{8,0},{9,1},... | collective-permute-start | bytes 98312 | tf_op jit(solution)/shard_map/ppermute | solution.py:212
  13.0 4.3 %collective-permute-start.2 = (f32[4,8,512]{2,1,0:T(8,128)S(1)}, f32[4,8,512]{2,1,0:T(8,128)S(1)}, u32[]{:S(2)}, u32[]{:S(2)}) collective-permute-start(f32[4,8,512]{2,1,0:T(8,128)S(1)} %pad_maximum_fusion.3), channel_id=1, source_target_pairs={{0,2},{1,3},{2,0},{3,1},{4,6},{5,7},{6,4},{7,5},{8,10},{9,11},{10,... | collective-permute-start | bytes 196616 | tf_op jit(solution)/shard_map/ppermute | solution.py:212
  17.3 1.4 %collective-permute-start.3 = (f32[8,8,512]{2,1,0:T(8,128)S(1)}, f32[8,8,512]{2,1,0:T(8,128)S(1)}, u32[]{:S(2)}, u32[]{:S(2)}) collective-permute-start(f32[8,8,512]{2,1,0:T(8,128)S(1)} %pad_maximum_fusion.2), channel_id=1, source_target_pairs={{0,1},{1,0},{2,3},{3,2},{4,5},{5,4},{6,7},{7,6},{8,9},{9,8},{10,11... | collective-permute-start | bytes 393224 | tf_op jit(solution)/shard_map/ppermute | solution.py:212
  21.6 1.6 %collective-permute-start.10 = (f32[4,136,128]{2,1,0:T(8,128)S(1)}, f32[4,136,128]{2,1,0:T(8,128)S(1)}, u32[]{:S(2)}, u32[]{:S(2)}) collective-permute-start(f32[4,136,128]{2,1,0:T(8,128)S(1)} %slice.59), channel_id=1, source_target_pairs={{0,1},{1,0},{2,3},{3,2},{4,5},{5,4},{6,7},{7,6},{8,9},{9,8},{10,11... | collective-permute-start | bytes 835592 | tf_op jit(solution)/shard_map/ppermute | solution.py:212
  23.3 5.1 %collective-permute-start.11 = (f32[2,136,128]{2,1,0:T(8,128)S(1)}, f32[2,136,128]{2,1,0:T(8,128)S(1)}, u32[]{:S(2)}, u32[]{:S(2)}) collective-permute-start(f32[2,136,128]{2,1,0:T(8,128)S(1)} %slice.75), channel_id=1, source_target_pairs={{0,2},{1,5},{2,0},{3,7},{4,6},{5,1},{6,4},{7,3},{8,10},{9,13},{10,... | collective-permute-start | bytes 417800 | tf_op jit(solution)/shard_map/ppermute | solution.py:212
  28.5 6.9 %collective-permute-start.12 = (f32[1,136,128]{2,1,0:T(8,128)S(1)}, f32[1,136,128]{2,1,0:T(8,128)S(1)}, u32[]{:S(2)}, u32[]{:S(2)}) collective-permute-start(f32[1,136,128]{2,1,0:T(8,128)S(1)} %slice.77), channel_id=1, source_target_pairs={{0,4},{1,3},{2,6},{3,1},{4,0},{5,7},{6,2},{7,5},{8,12},{9,11},{10,... | collective-permute-start | bytes 208904 | tf_op jit(solution)/shard_map/ppermute | solution.py:212
  35.2 1.6 %collective-permute-start.5 = (f32[8,8,512]{2,1,0:T(8,128)S(1)}, f32[8,8,512]{2,1,0:T(8,128)S(1)}, u32[]{:S(2)}, u32[]{:S(2)}) collective-permute-start(f32[8,8,512]{2,1,0:T(8,128)S(1)} %slice.65), channel_id=1, source_target_pairs={{0,1},{1,0},{2,3},{3,2},{4,5},{5,4},{6,7},{7,6},{8,9},{9,8},{10,11... | collective-permute-start | bytes 393224 | tf_op jit(solution)/shard_map/ppermute | solution.py:212
  35.3 6.9 %collective-permute-start.13 = (f32[1,136,128]{2,1,0:T(8,128)S(1)}, f32[1,136,128]{2,1,0:T(8,128)S(1)}, u32[]{:S(2)}, u32[]{:S(2)}) collective-permute-start(f32[1,136,128]{2,1,0:T(8,128)S(1)} %slice_add_fusion.4), channel_id=1, source_target_pairs={{0,8},{1,9},{2,10},{3,11},{4,12},{5,13},{6,14},{7,15},{8,0},{9,1},... | collective-permute-start | bytes 208904 | tf_op jit(solution)/shard_map/ppermute | solution.py:212
  36.9 6.9 %collective-permute-start.6 = (f32[4,8,512]{2,1,0:T(8,128)S(1)}, f32[4,8,512]{2,1,0:T(8,128)S(1)}, u32[]{:S(2)}, u32[]{:S(2)}) collective-permute-start(f32[4,8,512]{2,1,0:T(8,128)S(1)} %slice.67), channel_id=1, source_target_pairs={{0,2},{1,3},{2,0},{3,1},{4,6},{5,7},{6,4},{7,5},{8,10},{9,11},{10,... | collective-permute-start | bytes 196616 | tf_op jit(solution)/shard_map/ppermute | solution.py:212
  42.3 4.4 %collective-permute-start.14 = (f32[1,136,128]{2,1,0:T(8,128)S(1)}, f32[1,136,128]{2,1,0:T(8,128)S(1)}, u32[]{:S(2)}, u32[]{:S(2)}) collective-permute-start(f32[1,136,128]{2,1,0:T(8,128)S(1)} %add.38), channel_id=1, source_target_pairs={{0,16},{16,0},{1,17},{17,1},{2,18},{18,2},{3,19},{19,3},{4,20},{20... | collective-permute-start | bytes 208904 | tf_op jit(solution)/shard_map/ppermute | solution.py:212
  43.9 4.9 %collective-permute-start.7 = (f32[2,8,512]{2,1,0:T(8,128)S(1)}, f32[2,8,512]{2,1,0:T(8,128)S(1)}, u32[]{:S(2)}, u32[]{:S(2)}) collective-permute-start(f32[2,8,512]{2,1,0:T(8,128)S(1)} %slice.69), channel_id=1, source_target_pairs={{0,8},{1,9},{2,10},{3,11},{4,12},{5,13},{6,14},{7,15},{8,0},{9,1},... | collective-permute-start | bytes 98312 | tf_op jit(solution)/shard_map/ppermute | solution.py:212
  45.8 13.5 %collective-permute-start.9 = (f32[1,32,4096]{2,1,0:T(8,128)S(1)}, f32[1,32,4096]{2,1,0:T(8,128)S(1)}, u32[]{:S(2)}, u32[]{:S(2)}) collective-permute-start(f32[1,32,4096]{2,1,0:T(8,128)S(1)} %slice.73), channel_id=1, source_target_pairs={{0,16},{16,0},{1,17},{17,1},{2,18},{18,2},{3,19},{19,3},{4,20},{20... | collective-permute-start | bytes 1572872 | tf_op jit(solution)/shard_map/ppermute | solution.py:212
  46.7 4.5 %collective-permute-start.15 = (f32[1,136,128]{2,1,0:T(8,128)S(1)}, f32[1,136,128]{2,1,0:T(8,128)S(1)}, u32[]{:S(2)}, u32[]{:S(2)}) collective-permute-start(f32[1,136,128]{2,1,0:T(8,128)S(1)} %add.39), channel_id=1, source_target_pairs={{0,4},{1,3},{2,6},{3,1},{4,0},{5,7},{6,2},{7,5},{8,12},{9,11},{10,... | collective-permute-start | bytes 208904 | tf_op jit(solution)/shard_map/ppermute | solution.py:212
  48.8 4.0 %collective-permute-start.8 = (f32[1,8,512]{2,1,0:T(8,128)S(1)}, f32[1,8,512]{2,1,0:T(8,128)S(1)}, u32[]{:S(2)}, u32[]{:S(2)}) collective-permute-start(f32[1,8,512]{2,1,0:T(8,128)S(1)} %slice.71), channel_id=1, source_target_pairs={{0,4},{1,5},{2,6},{3,7},{4,0},{5,1},{6,2},{7,3},{8,12},{9,13},{10,... | collective-permute-start | bytes 49160 | tf_op jit(solution)/shard_map/ppermute | solution.py:212
  51.2 5.1 %collective-permute-start.16 = (f32[2,136,128]{2,1,0:T(8,128)S(1)}, f32[2,136,128]{2,1,0:T(8,128)S(1)}, u32[]{:S(2)}, u32[]{:S(2)}) collective-permute-start(f32[2,136,128]{2,1,0:T(8,128)S(1)} %pad_maximum_fusion.1), channel_id=1, source_target_pairs={{0,2},{1,5},{2,0},{3,7},{4,6},{5,1},{6,4},{7,3},{8,10},{9,13},{10,... | collective-permute-start | bytes 417800 | tf_op jit(solution)/shard_map/ppermute | solution.py:212
  56.3 3.9 %collective-permute-start.17 = (f32[4,136,128]{2,1,0:T(8,128)S(1)}, f32[4,136,128]{2,1,0:T(8,128)S(1)}, u32[]{:S(2)}, u32[]{:S(2)}) collective-permute-start(f32[4,136,128]{2,1,0:T(8,128)S(1)} %pad_maximum_fusion.refs_0_), channel_id=1, source_target_pairs={{0,1},{1,0},{2,3},{3,2},{4,5},{5,4},{6,7},{7,6},{8,9},{9,8},{10,11... | collective-permute-start | bytes 835592 | tf_op jit(solution)/shard_map/ppermute | solution.py:212

commit v4 on v3

--- a/solution.py
+++ b/solution.py
@@ -30,6 +30,8 @@
     n = len(parts)
     width = LANES // n
     block = lax.broadcasted_iota(jnp.int32, parts[0].shape, 1) // width
+    if n == 4:
+        return swap_four(parts, width, block)
     step = 1
     while step < n:
         low = (block & step) == 0
@@ -44,11 +46,33 @@
     return parts
 
 
+def swap_four(parts, width, block):
+    even, left, outer = (block & 1) == 0, block < 2, (block == 0) | (block == 3)
+    pairs = []
+    for p, r in (parts[:2], parts[2:]):
+        turned = pltpu.roll(jnp.where(even, r, p), width, 1)
+        pairs.append((jnp.where(even, p, turned), jnp.where(even, turned, r)))
+    (a, u), (b, v) = pairs
+    turned = pltpu.roll(jnp.where(left, b, a), 2 * width, 1)
+    kept = jnp.where(left, u, v)
+    other = pltpu.roll(jnp.where(left, v, u), 2 * width, 1)
+    return [
+        jnp.where(left, a, turned),
+        jnp.where(outer, other, kept),
+        jnp.where(left, turned, b),
+        jnp.where(outer, kept, other),
+    ]
+
+
 def place(m, order):
     p = 0
     for k, bit in enumerate(order):
         p = p | (((m >> bit) & 1) << k)
     return p
+
+
+def odd_tiles(n):
+    return (-(-n // 8) | 1) * 8
 
 
 class Dims:
@@ -65,6 +89,8 @@
         self.blk = side_a.shape[1]
         self.gb = self.blk // LANES
         self.per = self.Q // self.R
+        self.pairs = self.rows * self.cols
+        self.t_pitch, self.b_pitch, self.a_pitch = (odd_tiles(x) for x in (self.pairs, self.cols, self.rows))
         self.IC = self.rows * self.C
         self.JE = self.cols * self.C
 
@@ -78,9 +104,8 @@
 def pair_kernel(d, pg_ref, w_ref, t_ref, ph_ref, pl_ref, bias_ref, pv_ref, wv_ref, sems):
     w_copy = fetch(w_ref, wv_ref, sems.at[0])
     p_copy = fetch(pg_ref, pv_ref, sems.at[1])
-    pairs = d.rows * d.cols
     p_copy.wait()
-    flat = pv_ref[...].reshape(pairs, d.K)
+    flat = pv_ref[...].reshape(d.pairs, d.K)
     pg = split(flat)
     ph_ref[...], pl_ref[...] = split(flat.T)
     bias_ref[...] = jnp.broadcast_to(jnp.sum(flat, axis=0, keepdims=True), (8, d.K))
@@ -92,22 +117,27 @@
         )
         out = dot3(pg, split(w), NT)
         for v in range(two):
-            t_ref[pl.ds((u + v) * pairs, pairs), :] = out[:, v * LANES:(v + 1) * LANES]
+            t_ref[pl.ds(u + v, d.pairs, stride=d.G), :] = out[:, v * LANES:(v + 1) * LANES]
 
 
 def grad_outer_kernel(d, t_ref, gh_ref, gl_ref):
-    pairs = d.rows * d.cols
+    quads = range(d.cols // d.n)
     for i in range(d.rows):
-        for quad in range(d.cols // d.n):
-            parts = [t_ref[pl.ds(i * d.cols + quad * d.n + t, d.G, stride=pairs), :] for t in range(d.n)]
-            hi, lo = split(jnp.concatenate(swap_blocks(parts), axis=0))
+        at = i * d.cols
+        parts = [
+            jnp.concatenate([t_ref[pl.ds((at + quad * d.n + t) * d.G, d.G), :] for quad in quads], axis=0)
+            for t in range(d.n)
+        ]
+        done = swap_blocks(parts)
+        for quad in quads:
+            hi, lo = split(jnp.concatenate([x[quad * d.G:(quad + 1) * d.G] for x in done], axis=0))
             gh_ref[i * d.C:(i + 1) * d.C, quad * LANES:(quad + 1) * LANES] = hi
             gl_ref[i * d.C:(i + 1) * d.C, quad * LANES:(quad + 1) * LANES] = lo
 
 
 def own_right_kernel(d, b_ref, bh_ref, bl_ref, tb_ref, sem):
     copies = [
-        fetch(b_ref.at[:, pl.ds(v * LANES, LANES)], tb_ref.at[pl.ds(v * d.cols, d.cols)], sem) for v in range(d.g)
+        fetch(b_ref.at[:, pl.ds(v * LANES, LANES)], tb_ref.at[pl.ds(v * d.b_pitch, d.cols)], sem) for v in range(d.g)
     ]
     for copy in copies:
         copy.wait()
@@ -116,13 +146,13 @@
 
 def to_seq(d, b_ref, bh_ref, bl_ref, at, tb_ref):
     for v in range(d.g):
-        tb_ref[pl.ds(v * d.cols, d.cols), :] = b_ref[:, v * LANES:(v + 1) * LANES]
+        tb_ref[pl.ds(v * d.b_pitch, d.cols), :] = b_ref[:, v * LANES:(v + 1) * LANES]
     swap_to_seq(d, bh_ref, bl_ref, at, tb_ref)
 
 
 def swap_to_seq(d, bh_ref, bl_ref, at, tb_ref):
     for quad in range(d.cols // d.n):
-        parts = [tb_ref[pl.ds(quad * d.n + t, d.g, stride=d.cols), :] for t in range(d.n)]
+        parts = [tb_ref[pl.ds(quad * d.n + t, d.g, stride=d.b_pitch), :] for t in range(d.n)]
         hi, lo = split(jnp.concatenate(swap_blocks(parts), axis=0))
         bh_ref[at:at + d.slab, quad * LANES:(quad + 1) * LANES] = hi
         bl_ref[at:at + d.slab, quad * LANES:(quad + 1) * LANES] = lo
@@ -131,7 +161,6 @@
 def weight_kernel(d, order, blocks, ph_ref, pl_ref, bias_ref, a_ref, bx_ref, bh_ref, bl_ref, w_ref, ah_ref, al_ref, xh_ref, xl_ref,
                   t_ref, tb_ref, ta_ref, o_ref):
     r, q = lax.axis_index("row"), lax.axis_index("col")
-    pairs = d.rows * d.cols
     xh_ref[0:d.slab, :] = bh_ref[...]
     xl_ref[0:d.slab, :] = bl_ref[...]
     for m in range(1, d.R):
@@ -140,9 +169,9 @@
         for k in range(d.per):
             src = place(((r ^ m) * d.per + k) ^ q, order)
             for v in range(d.gb):
-                ta_ref[pl.ds((k * d.gb + v) * d.rows, d.rows), :] = a_ref[src, :, v * LANES:(v + 1) * LANES]
+                ta_ref[pl.ds((k * d.gb + v) * d.a_pitch, d.rows), :] = a_ref[src, :, v * LANES:(v + 1) * LANES]
         for quad in range(d.rows // d.n):
-            parts = [ta_ref[pl.ds(quad * d.n + t, d.g, stride=d.rows), :] for t in range(d.n)]
+            parts = [ta_ref[pl.ds(quad * d.n + t, d.g, stride=d.a_pitch), :] for t in range(d.n)]
             o_ref[m * d.slab:(m + 1) * d.slab, quad * LANES:(quad + 1) * LANES] = jnp.concatenate(
                 swap_blocks(parts), axis=0) * (1.0 / d.S)
     a = o_ref[0:d.S, 0:d.IC]
@@ -151,16 +180,22 @@
     al_ref[...] = lo
     o_ref[0:d.IC, :] = dot3(split(a.T), (xh_ref[...], xl_ref[...]), NN)
 
+    quads = range(d.cols // d.n)
     for i in range(d.rows):
-        for quad in range(d.cols // d.n):
-            parts = [o_ref[pl.ds(i * d.C + p4 * d.G, d.G), quad * LANES:(quad + 1) * LANES] for p4 in range(d.n)]
-            for t, x in enumerate(swap_blocks(parts)):
-                t_ref[pl.ds(i * d.cols + quad * d.n + t, d.G, stride=pairs), :] = x
+        parts = [
+            jnp.concatenate(
+                [o_ref[pl.ds(i * d.C + p4 * d.G, d.G), quad * LANES:(quad + 1) * LANES] for quad in quads], axis=0
+            )
+            for p4 in range(d.n)
+        ]
+        for t, x in enumerate(swap_blocks(parts)):
+            for quad in quads:
+                t_ref[pl.ds(i * d.cols + quad * d.n + t, d.G, stride=d.t_pitch), :] = x[quad * d.G:(quad + 1) * d.G]
     turned = ph_ref[...], pl_ref[...]
     keys = blocks.key(0), blocks.key(1)
     per = d.CE // blocks.count
     for u in range(d.G):
-        part = dot3(turned, split(t_ref[pl.ds(u * pairs, pairs), :]), NN).T
+        part = dot3(turned, split(t_ref[pl.ds(u * d.t_pitch, d.pairs), :]), NN).T
         for p4 in range(d.n):
             row = (p4 * d.G + u) * d.C
             block = row // per
@@ -177,9 +212,9 @@
         for quad in range(d.cols // d.n):
             parts = [o_ref[p * d.g:(p + 1) * d.g, quad * LANES:(quad + 1) * LANES] for p in range(d.n)]
             for t, x in enumerate(swap_blocks(parts)):
-                tb_ref[pl.ds(quad * d.n + t, d.g, stride=d.cols), :] = x
+                tb_ref[pl.ds(quad * d.n + t, d.g, stride=d.b_pitch), :] = x
         for v in range(d.g):
-            gb_ref[m, :, v * LANES:(v + 1) * LANES] = tb_ref[pl.ds(v * d.cols, d.cols), :]
+            gb_ref[m, :, v * LANES:(v + 1) * LANES] = tb_ref[pl.ds(v * d.b_pitch, d.cols), :]
 
 
 def left_grad_kernel(d, order, gh_ref, gl_ref, xh_ref, xl_ref, ga_ref, ta_ref):
@@ -191,11 +226,11 @@
         for quad in range(d.rows // d.n):
             parts = [out[p * d.g:(p + 1) * d.g, quad * LANES:(quad + 1) * LANES] for p in range(d.n)]
             for t, x in enumerate(swap_blocks(parts)):
-                ta_ref[pl.ds(quad * d.n + t, d.g, stride=d.rows), :] = x
+                ta_ref[pl.ds(quad * d.n + t, d.g, stride=d.a_pitch), :] = x
         for k in range(d.per):
             dst = place(((r ^ m) * d.per + k) ^ q, order)
             for v in range(d.gb):
-                ga_ref[dst, :, v * LANES:(v + 1) * LANES] = ta_ref[pl.ds((k * d.gb + v) * d.rows, d.rows), :]
+                ga_ref[dst, :, v * LANES:(v + 1) * LANES] = ta_ref[pl.ds((k * d.gb + v) * d.a_pitch, d.rows), :]
 
 
 def last_kernel(blocks, per, mine_ref, other_ref, w_ref, bias_ref):
@@ -272,8 +307,7 @@
         low = jnp.bfloat16
         taken, rest = plan(count)
         blocks = Blocks([bits for _, bits in taken])
-        pairs = d.rows * d.cols
-        t_s, tb_s, ta_s = (d.G * pairs, LANES), (d.g * d.cols, LANES), (d.g * d.rows, LANES)
+        t_s, tb_s, ta_s = (d.G * d.t_pitch, LANES), (d.g * d.b_pitch, LANES), (d.g * d.a_pitch, LANES)
         dma = pltpu.SemaphoreType.DMA
 
         left = side_a[None]
@@ -283,9 +317,9 @@
         for bit in range(count["row"]):
             right = double(right, "row", bit)
 
-        big, small, turn = shape(d.IC, d.JE, dtype=low), shape(d.slab, d.JE, dtype=low), shape(d.K, pairs, dtype=low)
+        big, small, turn = shape(d.IC, d.JE, dtype=low), shape(d.slab, d.JE, dtype=low), shape(d.K, d.pairs, dtype=low)
         outer, ph, plo, bias = call(
-            lambda *refs: pair_kernel(d, *refs), [shape(*t_s), turn, turn, shape(8, d.K)],
+            lambda *refs: pair_kernel(d, *refs), [shape(d.pairs * d.G, LANES), turn, turn, shape(8, d.K)],
             [(d.rows, d.cols, d.K), (d.CE, d.K), dma((2,))], hbm(pair_grad), hbm(out_weight), space=HBM,
         )
         gh, gl = call(lambda *refs: grad_outer_kernel(d, *refs), [big, big], [], outer)
@@ -325,7 +359,7 @@
 
 def plan(count):
     n = min(3, count["col"])
-    taken = [("col", (0, 0))] + [("col", (b, n - b)) for b in range(1, n)]
+    taken = [("col", (0, 0))] + [("col", (b, b)) for b in range(1, n)]
     rest = [("col", b) for b in range(n, count["col"])] + [("row", b) for b in range(count["row"])]
     return taken, rest
 

time: 61.3 us -> 56.1 us (0.915)
  Pallas kernels: 13.9 us -> 8.81 us
  waiting for transfers between devices: 22.4 us -> 18.9 us
  starting transfers between devices: 21.4 us -> 24.8 us
    pallas_call x7, Pallas kernels: 13.9 us -> 8.81 us  [call(): pl.pallas_call(kernel, out_shape=outs, in_specs=[pl.BlockSpec(memory_spac...]
    ppermute x18, waiting for transfers between devices: 22.4 us -> 18.9 us  [swap_with(): lax.ppermute(x, axis, [(i, i ^ 1 << bits[i & 1]) for i in range(size)])]
    ppermute x18, starting transfers between devices: 21.4 us -> 24.8 us  [swap_with(): lax.ppermute(x, axis, [(i, i ^ 1 << bits[i & 1]) for i in range(size)])]
  transfers between devices with their start and end apart: 18 -> 18, of which waited for: 11 -> 10; matrix products, arithmetic and copies ran while one was open for 4% -> 4% of each run, Pallas kernels for 17% -> 11%
where the time goes in v4:
time: 56.1 us; the launch traced here: 55.8 us
  starting transfers between devices  24.8 us (44%)
  waiting for transfers between devices  18.9 us (34%)
  Pallas kernels  8.81 us (16%)
  other arithmetic  2.38 us (4%)
  between operations  0.84 us (1%)
    ppermute x18, starting transfers between devices, swap_with(): lax.ppermute(x, axis, [(i, i ^ 1 << bits[i & 1]) for i in range(size)])  24.8 us
    ppermute x18, waiting for transfers between devices, swap_with(): lax.ppermute(x, axis, [(i, i ^ 1 << bits[i & 1]) for i in range(size)])  18.9 us
    pallas_call x7, Pallas kernels, call(): pl.pallas_call(kernel, out_shape=outs, in_specs=[pl.BlockSpec(memory_spac...  8.81 us
    squeeze x2, other arithmetic, local(): return (ga[0], gb[0], weight, bias)  1.49 us
  transfers between devices with their start and end apart: 18, of which 10 were waited for; matrix products, arithmetic and copies ran while one was open for 4% of the time, Pallas kernels for 11%

profile of v4, /device:TPU:0, one launch (start us, length us, event | category | flops | bytes accessed | tf_op | source)
XLA Modules:
  0.0 55.8 jit_solution(8205206899210879208)
XLA Ops:
  0.6 3.1 %collective-permute-start = (f32[1,8,512]{2,1,0:T(8,128)}, f32[1,8,512]{2,1,0:T(8,128)S(1)}, u32[]{:S(2)}, u32[]{:S(2)}) collective-permute-start(f32[1,8,512]{2,1,0:T(8,128)} %bitcast.8), channel_id=1, source_target_pairs={{0,4},{1,5},{2,6},{3,7},{4,0},{5,1},{6,2},{7,3},{8,12},{9,13},{10,... | collective-permute-start | bytes 49160 | tf_op jit(solution)/shard_map/ppermute | solution.py:247
  3.7 1.5 %collective-permute-start.4 = (f32[1,32,4096]{2,1,0:T(8,128)}, f32[1,32,4096]{2,1,0:T(8,128)S(1)}, u32[]{:S(2)}, u32[]{:S(2)}) collective-permute-start(f32[1,32,4096]{2,1,0:T(8,128)} %bitcast.7), channel_id=1, source_target_pairs={{0,16},{16,0},{1,17},{17,1},{2,18},{18,2},{3,19},{19,3},{4,20},{20... | collective-permute-start | bytes 1572872 | tf_op jit(solution)/shard_map/ppermute | solution.py:247
  6.4 3.0 %collective-permute-start.1 = (f32[2,8,512]{2,1,0:T(8,128)S(1)}, f32[2,8,512]{2,1,0:T(8,128)S(1)}, u32[]{:S(2)}, u32[]{:S(2)}) collective-permute-start(f32[2,8,512]{2,1,0:T(8,128)S(1)} %pad_maximum_fusion.4), channel_id=1, source_target_pairs={{0,8},{1,9},{2,10},{3,11},{4,12},{5,13},{6,14},{7,15},{8,0},{9,1},... | collective-permute-start | bytes 98312 | tf_op jit(solution)/shard_map/ppermute | solution.py:247
  9.4 1.3 %shard_map.77 = (bf16[128,1024]{1,0:T(8,128)(2,1)S(1)}, bf16[128,1024]{1,0:T(8,128)(2,1)S(1)}) custom-call(f32[32,4096]{1,0:T(8,128)} %refs_0_.3), custom_call_target="tpu_custom_call" | custom-call | tf_op jit(solution)/shard_map/pallas_call | solution.py:267
  10.8 1.8 %shard_map.75 = (f32[2048,128]{1,0:T(8,128)S(1)}, bf16[128,256]{1,0:T(8,128)(2,1)S(1)}, bf16[128,256]{1,0:T(8,128)(2,1)S(1)}, f32[8,128]{1,0:T(8,128)S(1)}) custom-call(f32[8,32,128]{2,1,0:T(8,128)} %refs_0_.2, f32[1024,128]{1,0:T(8,128)} %refs_1_.1), custom_call_target="tpu_custom_call" | custom-call | tf_op jit(solution)/shard_map/pallas_call | solution.py:267
  12.6 1.6 %collective-permute-start.2 = (f32[4,8,512]{2,1,0:T(8,128)S(1)}, f32[4,8,512]{2,1,0:T(8,128)S(1)}, u32[]{:S(2)}, u32[]{:S(2)}) collective-permute-start(f32[4,8,512]{2,1,0:T(8,128)S(1)} %pad_maximum_fusion.3), channel_id=1, source_target_pairs={{0,2},{1,3},{2,0},{3,1},{4,6},{5,7},{6,4},{7,5},{8,10},{9,11},{10,... | collective-permute-start | bytes 196616 | tf_op jit(solution)/shard_map/ppermute | solution.py:247
  14.1 2.8 %collective-permute-done.2 = f32[4,8,512]{2,1,0:T(8,128)S(1)} collective-permute-done((f32[4,8,512]{2,1,0:T(8,128)S(1)}, f32[4,8,512]{2,1,0:T(8,128)S(1)}, u32[]{:S(2)}, u32[]{:S(2)}) %collective-permute-start.2) | collective-permute-done | bytes 65568 | tf_op jit(solution)/shard_map/ppermute | solution.py:247
  17.0 1.3 %collective-permute-done.3 = f32[8,8,512]{2,1,0:T(8,128)S(1)} collective-permute-done((f32[8,8,512]{2,1,0:T(8,128)S(1)}, f32[8,8,512]{2,1,0:T(8,128)S(1)}, u32[]{:S(2)}, u32[]{:S(2)}) %collective-permute-start.3) | collective-permute-done | bytes 131104 | tf_op jit(solution)/shard_map/ppermute | solution.py:247
  18.4 2.0 %shard_map.78 = (f32[8,136,128]{2,1,0:T(8,128)S(1)}, bf16[256,256]{1,0:T(8,128)(2,1)S(1)}, bf16[256,256]{1,0:T(8,128)(2,1)S(1)}, bf16[256,1024]{1,0:T(8,128)(2,1)S(1)}, bf16[256,1024]{1,0:T(8,128)(2,1)S(1)}) custom-call(bf16[128,256]{1,0:T(8,128)(2,1)S(1)} %get-tuple-element.22.refs_0_, bf16[128,256]{1,0:T(8,128)(2,1)S(1)} %get-tuple-element.23.refs_1_, ...), custom_call_target="tpu_custom_call" | custom-call | tf_op jit(solution)/shard_map/pallas_call | solution.py:267
  20.6 1.4 %collective-permute-done.10 = f32[4,136,128]{2,1,0:T(8,128)S(1)} collective-permute-done((f32[4,136,128]{2,1,0:T(8,128)S(1)}, f32[4,136,128]{2,1,0:T(8,128)S(1)}, u32[]{:S(2)}, u32[]{:S(2)}) %collective-permute-start.10) | collective-permute-done | bytes 278560 | tf_op jit(solution)/shard_map/ppermute | solution.py:247
  22.0 1.6 %collective-permute-start.11 = (f32[2,136,128]{2,1,0:T(8,128)S(1)}, f32[2,136,128]{2,1,0:T(8,128)S(1)}, u32[]{:S(2)}, u32[]{:S(2)}) collective-permute-start(f32[2,136,128]{2,1,0:T(8,128)S(1)} %slice.75), channel_id=1, source_target_pairs={{0,2},{1,3},{2,0},{3,1},{4,6},{5,7},{6,4},{7,5},{8,10},{9,11},{10,... | collective-permute-start | bytes 417800 | tf_op jit(solution)/shard_map/ppermute | solution.py:247
  23.6 4.2 %collective-permute-done.11 = f32[2,136,128]{2,1,0:T(8,128)S(1)} collective-permute-done((f32[2,136,128]{2,1,0:T(8,128)S(1)}, f32[2,136,128]{2,1,0:T(8,128)S(1)}, u32[]{:S(2)}, u32[]{:S(2)}) %collective-permute-start.11) | collective-permute-done | bytes 139296 | tf_op jit(solution)/shard_map/ppermute | solution.py:247
  27.9 1.6 %collective-permute-start.12 = (f32[1,136,128]{2,1,0:T(8,128)S(1)}, f32[1,136,128]{2,1,0:T(8,128)S(1)}, u32[]{:S(2)}, u32[]{:S(2)}) collective-permute-start(f32[1,136,128]{2,1,0:T(8,128)S(1)} %slice.77), channel_id=1, source_target_pairs={{0,4},{1,5},{2,6},{3,7},{4,0},{5,1},{6,2},{7,3},{8,12},{9,13},{10,... | collective-permute-start | bytes 208904 | tf_op jit(solution)/shard_map/ppermute | solution.py:247
  30.2 1.3 %shard_map.79 = f32[16,8,512]{2,1,0:T(8,128)S(1)} custom-call(bf16[256,1024]{1,0:T(8,128)(2,1)S(1)} %get-tuple-element.20.refs_0_, bf16[256,1024]{1,0:T(8,128)(2,1)S(1)} %get-tuple-element.21.refs_1_, bf16[256,1024]{1,0:T(8,128)(2,1)S(1)} %get-tuple-element.27.refs_2_, bf16[256,1024]{1,0:T(8,128)(2,1)S(1)} %get-tuple-element.28.refs_3_), custom_call_target="tpu_custom_call" | custom-call | tf_op jit(solution)/shard_map/pallas_call | solution.py:267
  32.3 1.7 %collective-permute-start.13 = (f32[1,136,128]{2,1,0:T(8,128)S(1)}, f32[1,136,128]{2,1,0:T(8,128)S(1)}, u32[]{:S(2)}, u32[]{:S(2)}) collective-permute-start(f32[1,136,128]{2,1,0:T(8,128)S(1)} %slice_add_fusion.4), channel_id=1, source_target_pairs={{0,8},{1,9},{2,10},{3,11},{4,12},{5,13},{6,14},{7,15},{8,0},{9,1},... | collective-permute-start | bytes 208904 | tf_op jit(solution)/shard_map/ppermute | solution.py:247
  34.0 1.6 %collective-permute-start.6 = (f32[4,8,512]{2,1,0:T(8,128)S(1)}, f32[4,8,512]{2,1,0:T(8,128)S(1)}, u32[]{:S(2)}, u32[]{:S(2)}) collective-permute-start(f32[4,8,512]{2,1,0:T(8,128)S(1)} %slice.67), channel_id=1, source_target_pairs={{0,2},{1,3},{2,0},{3,1},{4,6},{5,7},{6,4},{7,5},{8,10},{9,11},{10,... | collective-permute-start | bytes 196616 | tf_op jit(solution)/shard_map/ppermute | solution.py:247
  35.5 2.3 %collective-permute-done.13 = f32[1,136,128]{2,1,0:T(8,128)S(1)} collective-permute-done((f32[1,136,128]{2,1,0:T(8,128)S(1)}, f32[1,136,128]{2,1,0:T(8,128)S(1)}, u32[]{:S(2)}, u32[]{:S(2)}) %collective-permute-start.13) | collective-permute-done | bytes 69664 | tf_op jit(solution)/shard_map/ppermute | solution.py:247
  37.9 1.6 %collective-permute-start.14 = (f32[1,136,128]{2,1,0:T(8,128)S(1)}, f32[1,136,128]{2,1,0:T(8,128)S(1)}, u32[]{:S(2)}, u32[]{:S(2)}) collective-permute-start(f32[1,136,128]{2,1,0:T(8,128)S(1)} %add.38), channel_id=1, source_target_pairs={{0,16},{16,0},{1,17},{17,1},{2,18},{18,2},{3,19},{19,3},{4,20},{20... | collective-permute-start | bytes 208904 | tf_op jit(solution)/shard_map/ppermute | solution.py:247
  39.5 1.4 %collective-permute-start.7 = (f32[2,8,512]{2,1,0:T(8,128)S(1)}, f32[2,8,512]{2,1,0:T(8,128)S(1)}, u32[]{:S(2)}, u32[]{:S(2)}) collective-permute-start(f32[2,8,512]{2,1,0:T(8,128)S(1)} %slice.69), channel_id=1, source_target_pairs={{0,8},{1,9},{2,10},{3,11},{4,12},{5,13},{6,14},{7,15},{8,0},{9,1},... | collective-permute-start | bytes 98312 | tf_op jit(solution)/shard_map/ppermute | solution.py:247
  42.4 2.2 %collective-permute-start.15 = (f32[1,136,128]{2,1,0:T(8,128)S(1)}, f32[1,136,128]{2,1,0:T(8,128)S(1)}, u32[]{:S(2)}, u32[]{:S(2)}) collective-permute-start(f32[1,136,128]{2,1,0:T(8,128)S(1)} %add.39), channel_id=1, source_target_pairs={{0,4},{1,5},{2,6},{3,7},{4,0},{5,1},{6,2},{7,3},{8,12},{9,13},{10,... | collective-permute-start | bytes 208904 | tf_op jit(solution)/shard_map/ppermute | solution.py:247
  44.6 1.3 %collective-permute-start.8 = (f32[1,8,512]{2,1,0:T(8,128)S(1)}, f32[1,8,512]{2,1,0:T(8,128)S(1)}, u32[]{:S(2)}, u32[]{:S(2)}) collective-permute-start(f32[1,8,512]{2,1,0:T(8,128)S(1)} %slice.71), channel_id=1, source_target_pairs={{0,4},{1,5},{2,6},{3,7},{4,0},{5,1},{6,2},{7,3},{8,12},{9,13},{10,... | collective-permute-start | bytes 49160 | tf_op jit(solution)/shard_map/ppermute | solution.py:247
  46.9 1.6 %collective-permute-start.16 = (f32[2,136,128]{2,1,0:T(8,128)S(1)}, f32[2,136,128]{2,1,0:T(8,128)S(1)}, u32[]{:S(2)}, u32[]{:S(2)}) collective-permute-start(f32[2,136,128]{2,1,0:T(8,128)S(1)} %pad_maximum_fusion.1), channel_id=1, source_target_pairs={{0,2},{1,3},{2,0},{3,1},{4,6},{5,7},{6,4},{7,5},{8,10},{9,11},{10,... | collective-permute-start | bytes 417800 | tf_op jit(solution)/shard_map/ppermute | solution.py:247
  49.1 2.9 %collective-permute-done.16 = f32[2,136,128]{2,1,0:T(8,128)S(1)} collective-permute-done((f32[2,136,128]{2,1,0:T(8,128)S(1)}, f32[2,136,128]{2,1,0:T(8,128)S(1)}, u32[]{:S(2)}, u32[]{:S(2)}) %collective-permute-start.16) | collective-permute-done | bytes 139296 | tf_op jit(solution)/shard_map/ppermute | solution.py:247
  52.1 1.9 %collective-permute-done.9 = f32[1,32,4096]{2,1,0:T(8,128)S(1)} collective-permute-done((f32[1,32,4096]{2,1,0:T(8,128)S(1)}, f32[1,32,4096]{2,1,0:T(8,128)S(1)}, u32[]{:S(2)}, u32[]{:S(2)}) %collective-permute-start.9) | collective-permute-done | bytes 524320 | tf_op jit(solution)/shard_map/ppermute | solution.py:247
  (49 shorter events, 7.8 us)
Async XLA Ops:
  0.6 5.0 %collective-permute-start = (f32[1,8,512]{2,1,0:T(8,128)}, f32[1,8,512]{2,1,0:T(8,128)S(1)}, u32[]{:S(2)}, u32[]{:S(2)}) collective-permute-start(f32[1,8,512]{2,1,0:T(8,128)} %bitcast.8), channel_id=1, source_target_pairs={{0,4},{1,5},{2,6},{3,7},{4,0},{5,1},{6,2},{7,3},{8,12},{9,13},{10,... | collective-permute-start | bytes 49160 | tf_op jit(solution)/shard_map/ppermute | solution.py:247
  3.7 5.7 %copy-start = (f32[8,512]{1,0:T(8,128)S(1)}, f32[8,512]{1,0:T(8,128)}, u32[]{:S(2)}) copy-start(f32[8,512]{1,0:T(8,128)} %param.4) | copy-start | bytes 49156
  3.7 14.6 %collective-permute-start.4 = (f32[1,32,4096]{2,1,0:T(8,128)}, f32[1,32,4096]{2,1,0:T(8,128)S(1)}, u32[]{:S(2)}, u32[]{:S(2)}) collective-permute-start(f32[1,32,4096]{2,1,0:T(8,128)} %bitcast.7), channel_id=1, source_target_pairs={{0,16},{16,0},{1,17},{17,1},{2,18},{18,2},{3,19},{19,3},{4,20},{20... | collective-permute-start | bytes 1572872 | tf_op jit(solution)/shard_map/ppermute | solution.py:247
  6.4 6.2 %collective-permute-start.1 = (f32[2,8,512]{2,1,0:T(8,128)S(1)}, f32[2,8,512]{2,1,0:T(8,128)S(1)}, u32[]{:S(2)}, u32[]{:S(2)}) collective-permute-start(f32[2,8,512]{2,1,0:T(8,128)S(1)} %pad_maximum_fusion.4), channel_id=1, source_target_pairs={{0,8},{1,9},{2,10},{3,11},{4,12},{5,13},{6,14},{7,15},{8,0},{9,1},... | collective-permute-start | bytes 98312 | tf_op jit(solution)/shard_map/ppermute | solution.py:247
  12.6 4.3 %collective-permute-start.2 = (f32[4,8,512]{2,1,0:T(8,128)S(1)}, f32[4,8,512]{2,1,0:T(8,128)S(1)}, u32[]{:S(2)}, u32[]{:S(2)}) collective-permute-start(f32[4,8,512]{2,1,0:T(8,128)S(1)} %pad_maximum_fusion.3), channel_id=1, source_target_pairs={{0,2},{1,3},{2,0},{3,1},{4,6},{5,7},{6,4},{7,5},{8,10},{9,11},{10,... | collective-permute-start | bytes 196616 | tf_op jit(solution)/shard_map/ppermute | solution.py:247
  16.9 1.4 %collective-permute-start.3 = (f32[8,8,512]{2,1,0:T(8,128)S(1)}, f32[8,8,512]{2,1,0:T(8,128)S(1)}, u32[]{:S(2)}, u32[]{:S(2)}) collective-permute-start(f32[8,8,512]{2,1,0:T(8,128)S(1)} %pad_maximum_fusion.2), channel_id=1, source_target_pairs={{0,1},{1,0},{2,3},{3,2},{4,5},{5,4},{6,7},{7,6},{8,9},{9,8},{10,11... | collective-permute-start | bytes 393224 | tf_op jit(solution)/shard_map/ppermute | solution.py:247
  20.4 1.6 %collective-permute-start.10 = (f32[4,136,128]{2,1,0:T(8,128)S(1)}, f32[4,136,128]{2,1,0:T(8,128)S(1)}, u32[]{:S(2)}, u32[]{:S(2)}) collective-permute-start(f32[4,136,128]{2,1,0:T(8,128)S(1)} %slice.59), channel_id=1, source_target_pairs={{0,1},{1,0},{2,3},{3,2},{4,5},{5,4},{6,7},{7,6},{8,9},{9,8},{10,11... | collective-permute-start | bytes 835592 | tf_op jit(solution)/shard_map/ppermute | solution.py:247
  22.0 5.8 %collective-permute-start.11 = (f32[2,136,128]{2,1,0:T(8,128)S(1)}, f32[2,136,128]{2,1,0:T(8,128)S(1)}, u32[]{:S(2)}, u32[]{:S(2)}) collective-permute-start(f32[2,136,128]{2,1,0:T(8,128)S(1)} %slice.75), channel_id=1, source_target_pairs={{0,2},{1,3},{2,0},{3,1},{4,6},{5,7},{6,4},{7,5},{8,10},{9,11},{10,... | collective-permute-start | bytes 417800 | tf_op jit(solution)/shard_map/ppermute | solution.py:247
  27.9 4.4 %collective-permute-start.12 = (f32[1,136,128]{2,1,0:T(8,128)S(1)}, f32[1,136,128]{2,1,0:T(8,128)S(1)}, u32[]{:S(2)}, u32[]{:S(2)}) collective-permute-start(f32[1,136,128]{2,1,0:T(8,128)S(1)} %slice.77), channel_id=1, source_target_pairs={{0,4},{1,5},{2,6},{3,7},{4,0},{5,1},{6,2},{7,3},{8,12},{9,13},{10,... | collective-permute-start | bytes 208904 | tf_op jit(solution)/shard_map/ppermute | solution.py:247
  31.6 2.4 %collective-permute-start.5 = (f32[8,8,512]{2,1,0:T(8,128)S(1)}, f32[8,8,512]{2,1,0:T(8,128)S(1)}, u32[]{:S(2)}, u32[]{:S(2)}) collective-permute-start(f32[8,8,512]{2,1,0:T(8,128)S(1)} %slice.65), channel_id=1, source_target_pairs={{0,1},{1,0},{2,3},{3,2},{4,5},{5,4},{6,7},{7,6},{8,9},{9,8},{10,11... | collective-permute-start | bytes 393224 | tf_op jit(solution)/shard_map/ppermute | solution.py:247
  32.3 5.6 %collective-permute-start.13 = (f32[1,136,128]{2,1,0:T(8,128)S(1)}, f32[1,136,128]{2,1,0:T(8,128)S(1)}, u32[]{:S(2)}, u32[]{:S(2)}) collective-permute-start(f32[1,136,128]{2,1,0:T(8,128)S(1)} %slice_add_fusion.4), channel_id=1, source_target_pairs={{0,8},{1,9},{2,10},{3,11},{4,12},{5,13},{6,14},{7,15},{8,0},{9,1},... | collective-permute-start | bytes 208904 | tf_op jit(solution)/shard_map/ppermute | solution.py:247
  34.0 5.5 %collective-permute-start.6 = (f32[4,8,512]{2,1,0:T(8,128)S(1)}, f32[4,8,512]{2,1,0:T(8,128)S(1)}, u32[]{:S(2)}, u32[]{:S(2)}) collective-permute-start(f32[4,8,512]{2,1,0:T(8,128)S(1)} %slice.67), channel_id=1, source_target_pairs={{0,2},{1,3},{2,0},{3,1},{4,6},{5,7},{6,4},{7,5},{8,10},{9,11},{10,... | collective-permute-start | bytes 196616 | tf_op jit(solution)/shard_map/ppermute | solution.py:247
  37.9 4.5 %collective-permute-start.14 = (f32[1,136,128]{2,1,0:T(8,128)S(1)}, f32[1,136,128]{2,1,0:T(8,128)S(1)}, u32[]{:S(2)}, u32[]{:S(2)}) collective-permute-start(f32[1,136,128]{2,1,0:T(8,128)S(1)} %add.38), channel_id=1, source_target_pairs={{0,16},{16,0},{1,17},{17,1},{2,18},{18,2},{3,19},{19,3},{4,20},{20... | collective-permute-start | bytes 208904 | tf_op jit(solution)/shard_map/ppermute | solution.py:247
  39.5 5.1 %collective-permute-start.7 = (f32[2,8,512]{2,1,0:T(8,128)S(1)}, f32[2,8,512]{2,1,0:T(8,128)S(1)}, u32[]{:S(2)}, u32[]{:S(2)}) collective-permute-start(f32[2,8,512]{2,1,0:T(8,128)S(1)} %slice.69), channel_id=1, source_target_pairs={{0,8},{1,9},{2,10},{3,11},{4,12},{5,13},{6,14},{7,15},{8,0},{9,1},... | collective-permute-start | bytes 98312 | tf_op jit(solution)/shard_map/ppermute | solution.py:247
  41.8 12.3 %collective-permute-start.9 = (f32[1,32,4096]{2,1,0:T(8,128)S(1)}, f32[1,32,4096]{2,1,0:T(8,128)S(1)}, u32[]{:S(2)}, u32[]{:S(2)}) collective-permute-start(f32[1,32,4096]{2,1,0:T(8,128)S(1)} %slice.73), channel_id=1, source_target_pairs={{0,16},{16,0},{1,17},{17,1},{2,18},{18,2},{3,19},{19,3},{4,20},{20... | collective-permute-start | bytes 1572872 | tf_op jit(solution)/shard_map/ppermute | solution.py:247
  42.4 4.5 %collective-permute-start.15 = (f32[1,136,128]{2,1,0:T(8,128)S(1)}, f32[1,136,128]{2,1,0:T(8,128)S(1)}, u32[]{:S(2)}, u32[]{:S(2)}) collective-permute-start(f32[1,136,128]{2,1,0:T(8,128)S(1)} %add.39), channel_id=1, source_target_pairs={{0,4},{1,5},{2,6},{3,7},{4,0},{5,1},{6,2},{7,3},{8,12},{9,13},{10,... | collective-permute-start | bytes 208904 | tf_op jit(solution)/shard_map/ppermute | solution.py:247
  44.6 3.8 %collective-permute-start.8 = (f32[1,8,512]{2,1,0:T(8,128)S(1)}, f32[1,8,512]{2,1,0:T(8,128)S(1)}, u32[]{:S(2)}, u32[]{:S(2)}) collective-permute-start(f32[1,8,512]{2,1,0:T(8,128)S(1)} %slice.71), channel_id=1, source_target_pairs={{0,4},{1,5},{2,6},{3,7},{4,0},{5,1},{6,2},{7,3},{8,12},{9,13},{10,... | collective-permute-start | bytes 49160 | tf_op jit(solution)/shard_map/ppermute | solution.py:247
  46.9 5.1 %collective-permute-start.16 = (f32[2,136,128]{2,1,0:T(8,128)S(1)}, f32[2,136,128]{2,1,0:T(8,128)S(1)}, u32[]{:S(2)}, u32[]{:S(2)}) collective-permute-start(f32[2,136,128]{2,1,0:T(8,128)S(1)} %pad_maximum_fusion.1), channel_id=1, source_target_pairs={{0,2},{1,3},{2,0},{3,1},{4,6},{5,7},{6,4},{7,5},{8,10},{9,11},{10,... | collective-permute-start | bytes 417800 | tf_op jit(solution)/shard_map/ppermute | solution.py:247
  52.1 2.9 %collective-permute-start.17 = (f32[4,136,128]{2,1,0:T(8,128)S(1)}, f32[4,136,128]{2,1,0:T(8,128)S(1)}, u32[]{:S(2)}, u32[]{:S(2)}) collective-permute-start(f32[4,136,128]{2,1,0:T(8,128)S(1)} %pad_maximum_fusion.refs_0_), channel_id=1, source_target_pairs={{0,1},{1,0},{2,3},{3,2},{4,5},{5,4},{6,7},{7,6},{8,9},{9,8},{10,11... | collective-permute-start | bytes 835592 | tf_op jit(solution)/shard_map/ppermute | solution.py:247
